TPU v7x, 32 devices: a whole 2x2x4 slice. The times are simulated.
32 devices in a mesh: dp: 8 (over z, y), head: 4 (over x, core).
Axes of the slice: x: 2, y: 2, z: 4, core: 2. Of those that a mesh axis runs over, the one named last changes fastest.
Arguments:
- features: bfloat16 [16, 64, 1024], P('dp', 'head'), may hold values from -6 to 6
- style_code: bfloat16 [16, 512], P('dp'), may hold values from -6 to 6
- labels: int32 [16], P('dp'), may hold values from 0 to 1023
- counts: int32 [8], P('dp'), may hold values from 1 to 2, as said below
- context: bfloat16 [16, 16, 1024], P('dp'), may hold values from -6 to 6
- noise_map: bfloat16 [16, 256], P('dp'), may hold values from -6 to 6
- w_select: bfloat16 [512, 8], P('dp'), may hold values from -0.5 to 0.5
- w_mod: bfloat16 [512, 1024], P('dp'), may hold values from -0.119628906 to 0.119628906
- kernel_bank: bfloat16 [8, 9, 1024, 1024], P(None, None, 'dp', 'head'), may hold values from -0.0625 to 0.0625
- conv_vecs: bfloat16 [2, 1024], P(None, 'dp'), may hold values from -3.5 to 3.5
- class_table: bfloat16 [1024, 1024], P('dp'), may hold values from -6 to 6
- w_qkv: bfloat16 [2, 1024, 1024], P(None, 'dp', 'head'), may hold values from -0.09375 to 0.09375
- w_attn_out: bfloat16 [1024, 1024], P('head', 'dp'), may hold values from -1 to 1
- w_cross_q: bfloat16 [1024, 1024], P('dp', 'head'), may hold values from -0.0625 to 0.0625
- w_cross_kv: bfloat16 [2, 1024, 1024], P(None, 'dp', 'head'), may hold values from -0.1875 to 0.1875
- w_cross_out: bfloat16 [1024, 1024], P('head', 'dp'), may hold values from -0.375 to 0.375
- w_mlp_in: bfloat16 [1024, 4096], P('dp', 'head'), may hold values from -0.1875 to 0.1875
- w_mlp_out: bfloat16 [4096, 1024], P('head', 'dp'), may hold values from -0.125 to 0.125
- w_rgb: bfloat16 [3, 1024], P(None, 'dp'), may hold values from -0.1875 to 0.1875
- cot_feat: bfloat16 [16, 256, 1024], P('dp', 'head'), may hold values from -6 to 6
- cot_rgb: bfloat16 [16, 3, 256], P('dp', None, 'head'), may hold values from -6 to 6
Outputs:
- features_out: bfloat16 [16, 256, 1024], P('dp', 'head')
- rgb_out: bfloat16 [16, 3, 256], P('dp', None, 'head')
- grad_input: float32 [16, 64, 1024], P('dp', 'head')
- grad_select: float32 [512, 8], P('dp')
- grad_mod: float32 [512, 1024], P('dp')
- grad_bank: float32 [8, 9, 1024, 1024], P(None, None, 'dp', 'head')
- grad_vecs: float32 [2, 1024], P(None, 'dp')
- grad_table: float32 [1024, 1024], P('dp')
- grad_qkv: float32 [2, 1024, 1024], P(None, 'dp', 'head')
- grad_attn_out: float32 [1024, 1024], P('head', 'dp')
- grad_cross_q: float32 [1024, 1024], P('dp', 'head')
- grad_cross_kv: float32 [2, 1024, 1024], P(None, 'dp', 'head')
- grad_cross_out: float32 [1024, 1024], P('head', 'dp')
- grad_mlp_in: float32 [1024, 4096], P('dp', 'head')
- grad_mlp_out: float32 [4096, 1024], P('head', 'dp')
- grad_rgb: float32 [3, 1024], P(None, 'dp')
Inputs may be any that keep to these rules, and one draw needn't show every extreme that they name: `counts`: each entry is the number of live slots of one index of dp; slots below it are live and the rest empty. At least one entry equals 2 in every draw.
All inputs are finite; a program needn't handle non-finite values.
Results may differ from a plain program's by a relative error of at most 0.03.
The roundings to bfloat16 on the way count: a program that leaves them out, or rounds other values in their place, can miss the bound.
Values may be sent and summed in bfloat16 or wider, within the bound.
No kernel may reach another device: no remote copies, remote signals or barrier semaphores. Data moves between devices by JAX's collectives and lax.ppermute only.
A program may use at most 512 MiB of HBM per device.

v0:
```python
from functools import partial

import jax
import jax.numpy as jnp
from jax import lax
from jax.sharding import PartitionSpec as P

D = 1024
DH = 64
KB = 8
RES = 16


HIGH = lax.Precision.HIGHEST
ROOT_TWO = 1.4142135623730951
SLOPE = 0.2
DEMOD_EPS = 1e-08


def leaky_relu(value):
    return jnp.where(value > 0, value, SLOPE * value) * ROOT_TWO


def gather_rows(piece):
    return lax.all_gather(piece, "head", axis=1, tiled=True)


def scatter_rows(partial_sum):
    return lax.psum_scatter(partial_sum, "head", scatter_dimension=1, tiled=True)


def split_heads(array):
    return array.reshape(array.shape[:-1] + (array.shape[-1] // DH, DH))


def join_heads(array):
    return array.reshape(array.shape[:-2] + (array.shape[-2] * array.shape[-1],))


def l2_scores(queries, keyset, score_scale):
    products = jnp.einsum("sphd,sqhd->shpq", queries, keyset, preferred_element_type=jnp.float32)
    key_square = jnp.sum(jnp.square(keyset.astype(jnp.float32)), axis=-1)
    return (2.0 * products - jnp.transpose(key_square, (0, 2, 1))[:, :, None, :]) * score_scale


def log_norm(scores):
    highest = jnp.max(scores, axis=-1, keepdims=True)
    return highest + jnp.log(jnp.sum(jnp.exp(scores - highest), axis=-1, keepdims=True))


def softmax_back(probs_full, dprobs):
    return probs_full * (dprobs - jnp.sum(probs_full * dprobs, axis=-1, keepdims=True))


def on_device(
    features,
    style_code,
    labels,
    counts,
    context,
    noise_map,
    w_select,
    w_mod,
    kernel_bank,
    conv_vecs,
    class_table,
    w_qkv,
    w_attn_out,
    w_cross_q,
    w_cross_kv,
    w_cross_out,
    w_mlp_in,
    w_mlp_out,
    w_rgb,
    cot_feat,
    cot_rgb,
):
    slot_count = features.shape[0]
    head_rank = lax.axis_index("head")
    width_own = w_qkv.shape[2]
    score_scale = DH ** (-0.5)
    (
        select_full,
        mod_full,
        vecs_full,
        table_full,
        qkv_full,
        attn_full,
        cross_q_full,
        cross_kv_full,
        cross_out_full,
        mlp_in_full,
        mlp_out_full,
        rgb_full,
        bank_full,
    ) = (
        lax.all_gather(w_select, "dp", axis=0, tiled=True),
        lax.all_gather(w_mod, "dp", axis=0, tiled=True),
        lax.all_gather(conv_vecs, "dp", axis=1, tiled=True),
        lax.all_gather(class_table, "dp", axis=0, tiled=True),
        lax.all_gather(w_qkv, "dp", axis=1, tiled=True),
        lax.all_gather(w_attn_out, "dp", axis=1, tiled=True),
        lax.all_gather(w_cross_q, "dp", axis=0, tiled=True),
        lax.all_gather(w_cross_kv, "dp", axis=1, tiled=True),
        lax.all_gather(w_cross_out, "dp", axis=1, tiled=True),
        lax.all_gather(w_mlp_in, "dp", axis=0, tiled=True),
        lax.all_gather(w_mlp_out, "dp", axis=1, tiled=True),
        lax.all_gather(w_rgb, "dp", axis=1, tiled=True),
        lax.all_gather(kernel_bank, "dp", axis=2, tiled=True),
    )
    mixing = jax.nn.softmax(
        jnp.dot(style_code, select_full, preferred_element_type=jnp.float32), axis=-1
    )
    mixing_low = mixing.astype(jnp.bfloat16)
    kernels = (
        jnp.dot(mixing_low, bank_full.reshape(KB, -1), preferred_element_type=jnp.float32)
        .astype(jnp.bfloat16)
        .reshape(slot_count, 9, D, width_own)
    )
    modulate = 1.0 + jnp.dot(style_code, mod_full, preferred_element_type=jnp.float32)
    kern_square = jnp.square(kernels.astype(jnp.float32))
    square_sum = jnp.einsum("stio,si->so", kern_square, jnp.square(modulate), precision=HIGH)
    demodulate = lax.rsqrt(square_sum + DEMOD_EPS)
    half_side = RES // 2
    grid_in = gather_rows(features).reshape(slot_count, half_side, half_side, D)
    upsampled = jnp.repeat(jnp.repeat(grid_in, 2, axis=1), 2, axis=2)
    modulated = (upsampled * modulate[:, None, None, :]).astype(jnp.bfloat16)
    padded = jnp.pad(modulated, ((0, 0), (1, 1), (1, 1), (0, 0)))
    conv_sum = jnp.zeros((slot_count, RES, RES, width_own), jnp.float32)
    for tap_index in range(9):
        row_off = tap_index // 3
        col_off = tap_index % 3
        conv_sum = conv_sum + jnp.einsum(
            "shwi,sio->shwo",
            padded[:, row_off : row_off + RES, col_off : col_off + RES],
            kernels[:, tap_index],
            preferred_element_type=jnp.float32,
        )
    conv_raw = conv_sum.reshape(slot_count, RES * RES, width_own)
    vecs_own = lax.dynamic_slice_in_dim(vecs_full, head_rank * width_own, width_own, 1).astype(
        jnp.float32
    )
    noise_full = noise_map.astype(jnp.float32)
    pre_act = conv_raw * demodulate[:, None, :] + vecs_own[0] * noise_full[:, :, None] + vecs_own[1]
    stream0 = lax.all_to_all(leaky_relu(pre_act), "head", split_axis=1, concat_axis=2, tiled=True)
    full0 = gather_rows(stream0.astype(jnp.bfloat16))
    qkv_own = jnp.einsum(
        "spi,nio->nspo", full0, qkv_full, preferred_element_type=jnp.float32
    ).astype(jnp.bfloat16)
    queries = split_heads(qkv_own[0])
    values_all = split_heads(qkv_own[1])
    scores = l2_scores(queries, queries, score_scale)
    self_norm = log_norm(scores)
    probs_low = jnp.exp(scores - self_norm).astype(jnp.bfloat16)
    attended = join_heads(
        jnp.einsum(
            "shpq,sqhd->sphd", probs_low, values_all, preferred_element_type=jnp.float32
        ).astype(jnp.bfloat16)
    )
    stream1 = stream0 + scatter_rows(
        jnp.einsum("spc,cd->spd", attended, attn_full, preferred_element_type=jnp.float32)
    )
    one_hot = (labels[:, None] == jnp.arange(table_full.shape[0], dtype=jnp.int32)[None, :]).astype(
        jnp.bfloat16
    )
    class_rows = jnp.dot(one_hot, table_full, preferred_element_type=jnp.float32)
    tokens = (context.astype(jnp.float32) + class_rows[:, None, :]).astype(jnp.bfloat16)
    cross_kv_own = jnp.einsum(
        "sci,nio->nsco", tokens, cross_kv_full, preferred_element_type=jnp.float32
    ).astype(jnp.bfloat16)
    ckeys = split_heads(cross_kv_own[0])
    cvalues = split_heads(cross_kv_own[1])
    full1 = gather_rows(stream1.astype(jnp.bfloat16))
    cqueries = split_heads(
        jnp.einsum("spi,io->spo", full1, cross_q_full, preferred_element_type=jnp.float32).astype(
            jnp.bfloat16
        )
    )
    cscores = (
        jnp.einsum("sphd,schd->shpc", cqueries, ckeys, preferred_element_type=jnp.float32)
        * score_scale
    )
    cross_norm = log_norm(cscores)
    cprobs_low = jnp.exp(cscores - cross_norm).astype(jnp.bfloat16)
    cout = join_heads(
        jnp.einsum(
            "shpc,schd->sphd", cprobs_low, cvalues, preferred_element_type=jnp.float32
        ).astype(jnp.bfloat16)
    )
    stream2 = stream1 + scatter_rows(
        jnp.einsum("spc,cd->spd", cout, cross_out_full, preferred_element_type=jnp.float32)
    )
    full2 = gather_rows(stream2.astype(jnp.bfloat16))
    hidden = jnp.einsum("spi,if->spf", full2, mlp_in_full, preferred_element_type=jnp.float32)
    active = jax.nn.gelu(hidden, approximate=True).astype(jnp.bfloat16)
    stream3 = stream2 + scatter_rows(
        jnp.einsum("spf,fd->spd", active, mlp_out_full, preferred_element_type=jnp.float32)
    )
    live_slots = (jnp.arange(slot_count, dtype=jnp.int32) < counts[0]).astype(jnp.float32)
    factor = live_slots / counts[0].astype(jnp.float32)
    features_out = (stream3 * live_slots[:, None, None]).astype(jnp.bfloat16)
    final_low = stream3.astype(jnp.bfloat16)
    colour = jnp.einsum("spi,ci->scp", final_low, rgb_full, preferred_element_type=jnp.float32)
    rgb_out = (colour * live_slots[:, None, None]).astype(jnp.bfloat16)
    rgb_weights = rgb_full.astype(jnp.float32)
    dcolour = cot_rgb.astype(jnp.float32) * factor[:, None, None]
    dstream = cot_feat.astype(jnp.float32) * factor[:, None, None] + jnp.einsum(
        "scp,ci->spi", dcolour, rgb_weights, precision=HIGH
    )
    rgb_grad_part = jnp.einsum(
        "scp,spi->ci", dcolour, final_low.astype(jnp.float32), precision=HIGH
    )
    dbranch = gather_rows(dstream.astype(jnp.bfloat16))
    mlp_out_grad = jnp.einsum("spf,spd->fd", active, dbranch, preferred_element_type=jnp.float32)
    dactive = jnp.einsum("spd,fd->spf", dbranch, mlp_out_full, preferred_element_type=jnp.float32)
    gelu_value, gelu_pull = jax.vjp(partial(jax.nn.gelu, approximate=True), hidden)
    dhidden = gelu_pull(dactive)[0].astype(jnp.bfloat16)
    mlp_in_grad = jnp.einsum("spi,spf->if", full2, dhidden, preferred_element_type=jnp.float32)
    dstream = dstream + scatter_rows(
        jnp.einsum("spf,if->spi", dhidden, mlp_in_full, preferred_element_type=jnp.float32)
    )
    dbranch = gather_rows(dstream.astype(jnp.bfloat16))
    cross_out_grad = jnp.einsum("spc,spd->cd", cout, dbranch, preferred_element_type=jnp.float32)
    dcout = split_heads(
        jnp.einsum(
            "spd,cd->spc", dbranch, cross_out_full, preferred_element_type=jnp.float32
        ).astype(jnp.bfloat16)
    )
    cprobs_full = jnp.exp(cscores - cross_norm)
    dcprobs = jnp.einsum("sphd,schd->shpc", dcout, cvalues, preferred_element_type=jnp.float32)
    dcvalues = jnp.einsum(
        "shpc,sphd->schd", cprobs_low, dcout, preferred_element_type=jnp.float32
    ).astype(jnp.bfloat16)
    dcscores = softmax_back(cprobs_full, dcprobs).astype(jnp.bfloat16)
    dcqueries = join_heads(
        (
            jnp.einsum("shpc,schd->sphd", dcscores, ckeys, preferred_element_type=jnp.float32)
            * score_scale
        ).astype(jnp.bfloat16)
    )
    dckeys = (
        jnp.einsum("shpc,sphd->schd", dcscores, cqueries, preferred_element_type=jnp.float32)
        * score_scale
    ).astype(jnp.bfloat16)
    cross_q_grad = jnp.einsum("spi,spo->io", full1, dcqueries, preferred_element_type=jnp.float32)
    dcross_kv = jnp.stack((join_heads(dckeys), join_heads(dcvalues)), axis=0)
    cross_kv_grad = jnp.einsum(
        "sci,nsco->nio", tokens, dcross_kv, preferred_element_type=jnp.float32
    )
    dtokens = jnp.einsum(
        "nsco,nio->sci", dcross_kv, cross_kv_full, preferred_element_type=jnp.float32
    )
    table_grad_part = jnp.dot(
        one_hot.astype(jnp.float32).T, jnp.sum(dtokens, axis=1), precision=HIGH
    )
    dstream = dstream + scatter_rows(
        jnp.einsum("spo,io->spi", dcqueries, cross_q_full, preferred_element_type=jnp.float32)
    )
    dbranch = gather_rows(dstream.astype(jnp.bfloat16))
    attn_out_grad = jnp.einsum("spc,spd->cd", attended, dbranch, preferred_element_type=jnp.float32)
    dattended = split_heads(
        jnp.einsum("spd,cd->spc", dbranch, attn_full, preferred_element_type=jnp.float32).astype(
            jnp.bfloat16
        )
    )
    probs_full = jnp.exp(l2_scores(queries, queries, score_scale) - self_norm)
    dprobs = jnp.einsum(
        "sphd,sqhd->shpq", dattended, values_all, preferred_element_type=jnp.float32
    )
    dvalues = jnp.einsum(
        "shpq,sphd->sqhd", probs_low, dattended, preferred_element_type=jnp.float32
    ).astype(jnp.bfloat16)
    dscores = softmax_back(probs_full, dprobs).astype(jnp.bfloat16)
    twice_scale = 2.0 * score_scale
    column_sums = jnp.transpose(jnp.sum(dscores.astype(jnp.float32), axis=2), (0, 2, 1))
    as_query = jnp.einsum("shpq,sqhd->sphd", dscores, queries, preferred_element_type=jnp.float32)
    as_key = jnp.einsum("shpq,sphd->sqhd", dscores, queries, preferred_element_type=jnp.float32)
    dshared = (
        (as_query + as_key - queries.astype(jnp.float32) * column_sums[..., None]) * twice_scale
    ).astype(jnp.bfloat16)
    dqkv = jnp.stack((join_heads(dshared), join_heads(dvalues)), axis=0)
    qkv_grad = jnp.einsum("spi,nspo->nio", full0, dqkv, preferred_element_type=jnp.float32)
    dstream = dstream + scatter_rows(
        jnp.einsum("nspo,nio->spi", dqkv, qkv_full, preferred_element_type=jnp.float32)
    )
    dconv_out = lax.all_to_all(
        dstream.astype(jnp.bfloat16), "head", split_axis=2, concat_axis=1, tiled=True
    ).astype(dstream.dtype)
    dpre = dconv_out * ROOT_TWO * jnp.where(pre_act > 0, 1.0, SLOPE)
    gain_grad = jnp.sum(dpre * noise_full[:, :, None], axis=(0, 1))
    bias_grad = jnp.sum(dpre, axis=(0, 1))
    vecs_grad_part = lax.dynamic_update_slice(
        jnp.zeros((2, D), jnp.float32),
        jnp.stack((gain_grad, bias_grad), axis=0),
        (0, head_rank * width_own),
    )
    ddemod = jnp.sum(dpre * conv_raw, axis=1)
    dconv = (
        (dpre * demodulate[:, None, :])
        .astype(jnp.bfloat16)
        .reshape(slot_count, RES, RES, width_own)
    )
    dpadded = jnp.zeros((slot_count, RES + 2, RES + 2, D), jnp.float32)
    tap_grads = []
    for tap_index in range(9):
        row_off = tap_index // 3
        col_off = tap_index % 3
        dpadded = dpadded.at[:, row_off : row_off + RES, col_off : col_off + RES].add(
            jnp.einsum(
                "shwo,sio->shwi", dconv, kernels[:, tap_index], preferred_element_type=jnp.float32
            )
        )
        tap_grads.append(
            jnp.einsum(
                "shwi,shwo->sio",
                padded[:, row_off : row_off + RES, col_off : col_off + RES],
                dconv,
                preferred_element_type=jnp.float32,
            )
        )
    dsquare = ddemod * -0.5 * demodulate * demodulate * demodulate
    dkernels = (
        jnp.stack(tap_grads, axis=1)
        + 2.0
        * kernels.astype(jnp.float32)
        * jnp.square(modulate)[:, None, :, None]
        * dsquare[:, None, None, :]
    )
    dkern_low = dkernels.astype(jnp.bfloat16)
    dmodulated = dpadded[:, 1 : RES + 1, 1 : RES + 1, :]
    dmodulate = jnp.sum(dmodulated * upsampled, axis=(1, 2)) + 2.0 * modulate * jnp.einsum(
        "stio,so->si", kern_square, dsquare, precision=HIGH
    )
    dupsampled = dmodulated * modulate[:, None, None, :]
    dgrid = jnp.sum(
        dupsampled.reshape(slot_count, half_side, 2, half_side, 2, D), axis=(2, 4)
    ).reshape(slot_count, half_side * half_side, D)
    grad_input = scatter_rows(dgrid)
    style_full = style_code.astype(jnp.float32)
    mod_grad_part = jnp.dot(style_full.T, dmodulate, precision=HIGH)
    bank_grad_part = jnp.dot(
        mixing_low.T, dkern_low.reshape(slot_count, -1), preferred_element_type=jnp.float32
    ).reshape(bank_full.shape)
    dmixing = jnp.dot(
        dkern_low.reshape(slot_count, -1),
        bank_full.reshape(KB, -1).T,
        preferred_element_type=jnp.float32,
    )
    logit_grad = mixing * (dmixing - jnp.sum(mixing * dmixing, axis=-1, keepdims=True))
    select_grad_part = jnp.dot(style_full.T, logit_grad, precision=HIGH)
    (
        grad_select,
        grad_mod,
        grad_vecs,
        grad_table,
        grad_qkv,
        grad_attn_out,
        grad_cross_q,
        grad_cross_kv,
        grad_cross_out,
        grad_mlp_in,
        grad_mlp_out,
        grad_rgb,
        grad_bank,
    ) = (
        lax.psum_scatter(select_grad_part, "dp", scatter_dimension=0, tiled=True),
        lax.psum_scatter(mod_grad_part, "dp", scatter_dimension=0, tiled=True),
        lax.psum_scatter(vecs_grad_part, "dp", scatter_dimension=1, tiled=True),
        lax.psum_scatter(table_grad_part, "dp", scatter_dimension=0, tiled=True),
        lax.psum_scatter(qkv_grad, "dp", scatter_dimension=1, tiled=True),
        lax.psum_scatter(attn_out_grad, "dp", scatter_dimension=1, tiled=True),
        lax.psum_scatter(cross_q_grad, "dp", scatter_dimension=0, tiled=True),
        lax.psum_scatter(cross_kv_grad, "dp", scatter_dimension=1, tiled=True),
        lax.psum_scatter(cross_out_grad, "dp", scatter_dimension=1, tiled=True),
        lax.psum_scatter(mlp_in_grad, "dp", scatter_dimension=0, tiled=True),
        lax.psum_scatter(mlp_out_grad, "dp", scatter_dimension=1, tiled=True),
        lax.psum_scatter(rgb_grad_part, "dp", scatter_dimension=1, tiled=True),
        lax.psum_scatter(bank_grad_part, "dp", scatter_dimension=2, tiled=True),
    )
    grad_select, grad_mod, grad_vecs, grad_table, grad_rgb = (
        lax.psum(grad_select.astype(jnp.bfloat16), "head").astype(jnp.float32),
        lax.psum(grad_mod.astype(jnp.bfloat16), "head").astype(jnp.float32),
        lax.psum(grad_vecs.astype(jnp.bfloat16), "head").astype(jnp.float32),
        lax.psum(grad_table.astype(jnp.bfloat16), "head").astype(jnp.float32),
        lax.psum(grad_rgb.astype(jnp.bfloat16), "head").astype(jnp.float32),
    )
    return (
        features_out,
        rgb_out,
        grad_input,
        grad_select,
        grad_mod,
        grad_bank,
        grad_vecs,
        grad_table,
        grad_qkv,
        grad_attn_out,
        grad_cross_q,
        grad_cross_kv,
        grad_cross_out,
        grad_mlp_in,
        grad_mlp_out,
        grad_rgb,
    )


def solution(mesh):
    return jax.shard_map(
        on_device,
        mesh=mesh,
        in_specs=(
            P("dp", "head", None),
            P("dp", None),
            P("dp"),
            P("dp"),
            P("dp", None, None),
            P("dp", None),
            P("dp", None),
            P("dp", None),
            P(None, None, "dp", "head"),
            P(None, "dp"),
            P("dp", None),
            P(None, "dp", "head"),
            P("head", "dp"),
            P("dp", "head"),
            P(None, "dp", "head"),
            P("head", "dp"),
            P("dp", "head"),
            P("head", "dp"),
            P(None, "dp"),
            P("dp", "head", None),
            P("dp", None, "head"),
        ),
        out_specs=(
            P("dp", "head", None),
            P("dp", None, "head"),
            P("dp", "head", None),
            P("dp", None),
            P("dp", None),
            P(None, None, "dp", "head"),
            P(None, "dp"),
            P("dp", None),
            P(None, "dp", "head"),
            P("head", "dp"),
            P("dp", "head"),
            P(None, "dp", "head"),
            P("head", "dp"),
            P("dp", "head"),
            P("head", "dp"),
            P(None, "dp"),
        ),
        check_vma=False,
    )
```

profile of v0, /device:TPU:0, one launch (start us, length us, event | category | flops | bytes accessed | tf_op | source)
XLA Modules:
  0.0 3505.4 jit_solution(6537250915783115919)
XLA Ops:
  8.0 7.5 copy.135
  18.0 22.2 all_gather.64
  40.8 73.6 %all-gather = bf16[8,64,8]{1,2,0:T(8,128)(2,1)S(1)} all-gather(bf16[1,64,8]{1,2,0:T(8,128)(2,1)S(1)} %bitcast.522), channel_id=1, replica_groups=mesh['dp'=8,'head'=4] {'dp'}, dimensions={0}, use_global_device_ids=true | all-gather | bytes 9216 | tf_op jit(solution)/shard_map/all_gather | solution.py:97
  114.4 5.8 all_gather.60
  128.4 642.1 %all-gather.17.cloned.1.call-done = bf16[8,9,1024,256]{3,0,2,1:T(8,128)(2,1)} async-done(((bf16[8,9,128,256]{3,0,2,1:T(8,128)(2,1)}), bf16[8,9,1024,256]{3,0,2,1:T(8,128)(2,1)}) %all-gather.17.cloned.1.call-update) | async-done | bytes 37748752 | tf_op jit(solution)/shard_map/all_gather | solution.py:109
  770.5 19.4 convolution_convert_fusion
  789.9 6.2 copy.245
  806.2 11.7 all_to_all.27
  819.4 28.9 all_gather.67
  856.3 27.2 reduce-scatter.32.cloned.1.call-done
  886.6 30.2 all_gather.71
  916.7 31.4 all_gather.72
  950.2 37.3 %all-gather.25.cloned.1.call-done = bf16[2,1024,256]{2,1,0:T(8,128)(2,1)} async-done(((bf16[2,128,256]{2,1,0:T(8,128)(2,1)}), bf16[2,1024,256]{2,1,0:T(8,128)(2,1)}) %all-gather.25.cloned.1.call-update) | async-done | bytes 1048592 | tf_op jit(solution)/shard_map/all_gather | solution.py:104
  989.1 16.0 all-gather.27.cloned.1.call-done
  1010.4 30.9 reduce-scatter.34.cloned.1.call-done
  1044.2 20.7 all_gather.76
  1067.2 25.4 all-gather.31.cloned.1.call-done
  1092.6 17.4 all-gather.29.cloned.1.call-done
  1110.0 4.5 fusion.21
  1114.5 14.3 all-gather.35.cloned.1.call-done
  1128.8 53.2 %all-gather.33.cloned.1.call-done = bf16[1024,1024]{1,0:T(8,128)(2,1)} async-done(((bf16[1024,128]{1,0:T(8,128)(2,1)}), bf16[1024,1024]{1,0:T(8,128)(2,1)}) %all-gather.33.cloned.1.call-update) | async-done | bytes 2097168 | tf_op jit(solution)/shard_map/all_gather | solution.py:107
  1181.9 5.0 fusion.12
  1190.6 29.7 reduce-scatter.38.cloned.1.call-done
  1222.6 16.8 all-gather.37.cloned.1.call-done
  1245.7 31.1 reduce-scatter.40.cloned.1.call-done
  1279.1 16.8 all-gather.39.cloned.1.call-done
  1309.0 4.3 fusion.17
  1315.4 4.0 fusion.88
  1320.0 19.0 reduce-scatter.42.cloned.1.call-done
  1346.8 4.4 all-to-all-done.1
  1355.6 4.3 dynamic-slice_add_fusion
  1359.8 10.1 scatter-add.31
  1369.9 5.0 add_select_fusion
  1375.0 10.1 scatter-add.34
  1390.1 8.9 scatter-add.36
  1402.1 8.9 scatter-add.39
  1416.1 8.9 scatter-add.41
  1428.1 8.9 scatter-add.44
  1454.2 8.1 mul.393.clone
  1462.3 32.0 copy.247
  1518.5 12.5 fusion.3
  1531.5 36.6 %multiply_reduce_fusion.5 = (f32[2]{0:T(128)S(1)}, f32[2,8]{1,0:T(2,128)S(1)}) fusion(bf16[8,9,1024,256]{3,0,2,1:T(8,128)(2,1)} %all-gather.17.cloned.1.call-done, bf16[2,9,1024,256]{3,2,0,1:T(8,128)(2,1)} %fusion.3, f32[2]{0:T(128)S(1)} %copy-done.80, f32[2,8]{1,0:T(2,128)S(1)} %copy-done.70, f32[2]{0:T(128)S(1)} %copy-done.78), kind=kOutput, calls=%fused_computation.219 | convolution fusion | flops 75497536 | bytes 47186072 | tf_op jit(solution)/shard_map/dot_general | solution.py:344
  1568.3 7.5 copy.172
  1575.8 8.3 mul.401.clone
  1584.1 31.9 copy.248
  1616.0 51.9 %copy.246 = f32[1,2,9216,256]{3,1,2,0:T(2,128)} copy(f32[1,2,9216,256]{3,2,1,0:T(8,128)S(1)} %bitcast.457) | data formatting | bytes 37748736
  1668.8 25.0 add_convert_fusion
  1695.7 29.0 fusion.103
  1724.7 50.2 %copy.235 = f32[8,9,1024,256]{3,0,1,2:T(8,128)} copy(f32[8,9,1024,256]{3,0,2,1:T(8,128)} %fusion.103) | data formatting | bytes 150994944
  1774.8 51.6 %copy.249 = f32[128,8,72,256]{3,1,2,0:T(8,128)} copy(f32[128,8,72,256]{3,2,1,0:T(8,128)} %bitcast.193) | data formatting | bytes 150994944
  1830.8 5.1 convolution_bitcast_fusion
  1845.9 4.0 reduce_sum.151
  1856.1 15.6 reduce-scatter.62.cloned.1.call-done
  1872.5 5.6 all-reduce.2
  1879.9 26.5 all-reduce.6.cloned.1.call-done
  1910.0 1178.9 %reduce-scatter.66.cloned.1.call-done = f32[128,18432]{1,0:T(8,128)} async-done(((f32[1024,18432]{1,0:T(8,128)}), f32[128,18432]{1,0:T(8,128)}) %reduce-scatter.66.cloned.1.call-update) | async-done | bytes 9437200
  3088.9 6.6 copy.250
  3095.5 6.6 copy.184
  3102.1 53.9 %reduce-scatter.56.cloned.1.call-done = f32[256,128]{1,0:T(8,128)} async-done(((f32[256,1024]{1,0:T(8,128)}), f32[256,128]{1,0:T(8,128)}) %reduce-scatter.56.cloned.1.call-update) | async-done | bytes 131088 | tf_op jit(solution)/shard_map/reduce_scatter | solution.py:374
  3156.0 66.6 %reduce-scatter.52.cloned.1.call-done = f32[128,256]{1,0:T(8,128)} async-done(((f32[1024,256]{1,0:T(8,128)}), f32[128,256]{1,0:T(8,128)}) %reduce-scatter.52.cloned.1.call-update) | async-done | bytes 131088 | tf_op jit(solution)/shard_map/reduce_scatter | solution.py:372
  3222.7 91.7 %reduce-scatter.60.cloned.1.call-done = f32[1024,128]{1,0:T(8,128)} async-done(((f32[1024,1024]{1,0:T(8,128)}), f32[1024,128]{1,0:T(8,128)}) %reduce-scatter.60.cloned.1.call-update) | async-done | bytes 524304 | tf_op jit(solution)/shard_map/reduce_scatter | solution.py:376
  3314.4 92.5 %reduce-scatter.58.cloned.1.call-done = f32[128,1024]{1,0:T(8,128)} async-done(((f32[1024,1024]{1,0:T(8,128)}), f32[128,1024]{1,0:T(8,128)}) %reduce-scatter.58.cloned.1.call-update) | async-done | bytes 524304 | tf_op jit(solution)/shard_map/reduce_scatter | solution.py:375
  3406.9 67.5 %reduce-scatter.50.cloned.1.call-done = f32[256,128]{1,0:T(8,128)} async-done(((f32[256,1024]{1,0:T(8,128)}), f32[256,128]{1,0:T(8,128)}) %reduce-scatter.50.cloned.1.call-update) | async-done | bytes 131088 | tf_op jit(solution)/shard_map/reduce_scatter | solution.py:371
  3474.4 23.9 reduce-scatter.44.cloned.1.call-done
  (427 shorter events, 177.0 us)
Async XLA Ops:
  7.2 118.1 %copy-start = (bf16[2,512]{1,0:T(2,128)(2,1)S(1)}, bf16[2,512]{1,0:T(2,128)(2,1)}, u32[]{:S(2)}) copy-start(bf16[2,512]{1,0:T(2,128)(2,1)} %param.40) | copy-start | bytes 6148
  7.2 118.5 %all-gather.15.cloned.1.call-start = ((), (), s32[]{:S(2)}) async-start(), calls=%async_computation.22 | async-start | bytes 1179648 | tf_op jit(solution)/shard_map/all_gather | solution.py:98
  7.9 762.6 %all-gather.17.cloned.1.call-start = ((), (), s32[]{:S(2)}) async-start(), calls=%async_computation.23 | async-start | bytes 42467328 | tf_op jit(solution)/shard_map/all_gather | solution.py:109
  15.4 25.3 copy-start.85
  15.5 99.0 %copy-start.59 = (bf16[2,16,1024]{2,1,0:T(8,128)(2,1)S(1)}, bf16[2,16,1024]{2,1,0:T(8,128)(2,1)}, u32[]{:S(2)}) copy-start(bf16[2,16,1024]{2,1,0:T(8,128)(2,1)} %param.39) | copy-start | bytes 196612
  15.5 832.8 %all-gather.21.cloned.1.call-start = ((), (), s32[]{:S(2)}) async-start(), calls=%async_computation.25 | async-start | bytes 1179648 | tf_op jit(solution)/shard_map/all_gather | solution.py:101
  17.1 831.2 %all-gather.19.cloned.1.call-start = ((), (), s32[]{:S(2)}) async-start(), calls=%async_computation.24 | async-start | bytes 1310720 | tf_op jit(solution)/shard_map/all_gather | solution.py:25
  40.8 764.7 %copy-start.73 = (f32[1,256]{1,0:T(1,128)}, f32[1,256]{1,0:T(1,128)S(1)}, u32[]{:S(2)}) copy-start(f32[1,256]{1,0:T(1,128)S(1)} %get-tuple-element.201) | copy-start | bytes 3076
  125.5 645.0 %copy-start.69 = (f32[2,8]{1,0:T(2,128)}, f32[2,8]{1,0:T(2,128)S(1)}, u32[]{:S(2)}) copy-start(f32[2,8]{1,0:T(2,128)S(1)} %get-tuple-element.208) | copy-start | bytes 196
  125.5 645.0 %copy-start.77 = (f32[2]{0:T(128)}, f32[2]{0:T(128)S(1)}, u32[]{:S(2)}) copy-start(f32[2]{0:T(128)S(1)} %get-tuple-element.207) | copy-start | bytes 28
  125.7 644.8 %copy-start.79 = (f32[2]{0:T(128)}, f32[2]{0:T(128)S(1)}, u32[]{:S(2)}) copy-start(f32[2]{0:T(128)S(1)} %fusion.102) | copy-start | bytes 28
  128.4 674.0 %copy-start.35 = (bf16[2,16,16,1024]{3,2,1,0:T(8,128)(2,1)}, bf16[2,16,16,1024]{3,2,1,0:T(8,128)(2,1)S(1)}, u32[]{:S(2)}) copy-start(bf16[2,16,16,1024]{3,2,1,0:T(8,128)(2,1)S(1)} %multiply_convert_fusion.2) | copy-start | bytes 3145732
  805.5 547.1 %copy-start.13 = (f32[2,16,16,256]{3,2,1,0:T(8,128)}, f32[2,16,16,256]{3,2,1,0:T(8,128)S(1)}, u32[]{:S(2)}) copy-start(f32[2,16,16,256]{3,2,1,0:T(8,128)S(1)} %get-tuple-element.220) | copy-start | bytes 1572868
  806.2 13.2 copy-start.60
  819.3 64.2 %reduce-scatter.32.cloned.1.call-start = ((), (), s32[]{:S(2)}) async-start(), calls=%async_computation.26 | async-start | bytes 2621440 | tf_op jit(solution)/shard_map/reduce_scatter | solution.py:29
  854.9 93.3 %copy-start.81 = (s32[2]{0:T(128)S(1)}, s32[2]{0:T(128)}, u32[]{:S(2)}) copy-start(s32[2]{0:T(128)} %param.41) | copy-start | bytes 28
  854.9 93.3 %all-gather.23.cloned.1.call-start = ((), (), s32[]{:S(2)}) async-start(), calls=%async_computation.27 | async-start | bytes 2359296 | tf_op jit(solution)/shard_map/all_gather | solution.py:100
  855.5 132.0 %all-gather.25.cloned.1.call-start = ((), (), s32[]{:S(2)}) async-start(), calls=%async_computation.28 | async-start | bytes 1179648 | tf_op jit(solution)/shard_map/all_gather | solution.py:104
  856.2 148.9 %all-gather.27.cloned.1.call-start = ((), (), s32[]{:S(2)}) async-start(), calls=%async_computation.29 | async-start | bytes 1310720 | tf_op jit(solution)/shard_map/all_gather | solution.py:25
  885.5 101.9 %copy-start.46 = (bf16[2,16,1024]{2,1,0:T(8,128)(2,1)S(1)}, bf16[2,16,1024]{2,1,0:T(8,128)(2,1)}, u32[]{:S(2)}) copy-start(bf16[2,16,1024]{2,1,0:T(8,128)(2,1)} %param.43) | copy-start | bytes 196612
  885.6 155.7 %reduce-scatter.34.cloned.1.call-start = ((), (), s32[]{:S(2)}) async-start(), calls=%async_computation.30 | async-start | bytes 2621440 | tf_op jit(solution)/shard_map/reduce_scatter | solution.py:29
  916.7 90.2 %copy-start.33 = (bf16[1024,256]{0,1:T(8,128)(2,1)}, bf16[1024,256]{0,1:T(8,128)(2,1)S(1)}, u32[]{:S(2)}) copy-start(bf16[1024,256]{0,1:T(8,128)(2,1)S(1)} %all_gather.71) | copy-start | bytes 1572868
  950.2 57.8 %copy-start.54 = (f32[2,1024]{1,0:T(2,128)}, f32[2,1024]{1,0:T(2,128)S(1)}, u32[]{:S(2)}) copy-start(f32[2,1024]{1,0:T(2,128)S(1)} %fusion.89) | copy-start | bytes 24580
  1009.7 34.5 copy-start.87
  1009.7 55.2 %copy-start.86 = (bf16[2,3,64]{2,0,1:T(2,128)(2,1)S(1)}, bf16[2,3,64]{2,0,1:T(2,128)(2,1)}, u32[]{:S(2)}) copy-start(bf16[2,3,64]{2,0,1:T(2,128)(2,1)} %param.59) | copy-start | bytes 2308
  1009.7 82.9 %all-gather.31.cloned.1.call-start = ((), (), s32[]{:S(2)}) async-start(), calls=%async_computation.32 | async-start | bytes 2359296 | tf_op jit(solution)/shard_map/all_gather | solution.py:106
  1009.8 55.2 %copy-start.48 = (bf16[2,64,1024]{2,1,0:T(8,128)(2,1)S(1)}, bf16[2,64,1024]{2,1,0:T(8,128)(2,1)}, u32[]{:S(2)}) copy-start(bf16[2,64,1024]{2,1,0:T(8,128)(2,1)} %param.58) | copy-start | bytes 786436
  1010.3 99.7 %all-gather.29.cloned.1.call-start = ((), (), s32[]{:S(2)}) async-start(), calls=%async_computation.31 | async-start | bytes 1310720 | tf_op jit(solution)/shard_map/all_gather | solution.py:25
  1043.5 85.3 %all-gather.35.cloned.1.call-start = ((), (), s32[]{:S(2)}) async-start(), calls=%async_computation.35 | async-start | bytes 1310720 | tf_op jit(solution)/shard_map/all_gather | solution.py:25
  1064.9 49.6 %copy-start.56 = (bf16[3,1024]{1,0:T(4,128)(2,1)}, bf16[3,1024]{1,0:T(4,128)(2,1)S(1)}, u32[]{:S(2)}) copy-start(bf16[3,1024]{1,0:T(4,128)(2,1)S(1)} %all_gather.76) | copy-start | bytes 18436
  1066.4 115.5 %all-gather.33.cloned.1.call-start = ((), (), s32[]{:S(2)}) async-start(), calls=%async_computation.33 | async-start | bytes 2359296 | tf_op jit(solution)/shard_map/all_gather | solution.py:107
  1067.1 153.2 %reduce-scatter.38.cloned.1.call-start = ((), (), s32[]{:S(2)}) async-start(), calls=%async_computation.36 | async-start | bytes 2621440 | tf_op jit(solution)/shard_map/reduce_scatter | solution.py:29
  1190.6 48.8 %all-gather.37.cloned.1.call-start = ((), (), s32[]{:S(2)}) async-start(), calls=%async_computation.37 | async-start | bytes 1310720 | tf_op jit(solution)/shard_map/all_gather | solution.py:25
  1222.5 54.3 %reduce-scatter.40.cloned.1.call-start = ((), (), s32[]{:S(2)}) async-start(), calls=%async_computation.38 | async-start | bytes 2621440 | tf_op jit(solution)/shard_map/reduce_scatter | solution.py:29
  1245.3 52.5 %copy-start.50 = (f32[1,8,256]{2,1,0:T(8,128)S(1)}, f32[1,8,256]{2,1,0:T(8,128)}, u32[]{:S(2)}) copy-start(f32[1,8,256]{2,1,0:T(8,128)} %copy-done.49) | copy-start | bytes 24580
  1245.3 50.6 %all-gather.39.cloned.1.call-start = ((), (), s32[]{:S(2)}) async-start(), calls=%async_computation.39 | async-start | bytes 1310720 | tf_op jit(solution)/shard_map/all_gather | solution.py:25
  1279.0 19.9 copy-start.21
  1279.0 60.0 %reduce-scatter.42.cloned.1.call-start = ((), (), s32[]{:S(2)}) async-start(), calls=%async_computation.40 | async-start | bytes 2621440 | tf_op jit(solution)/shard_map/reduce_scatter | solution.py:29
  1307.5 139.4 %reduce-scatter.36.cloned.1.call-start = ((), (), s32[]{:S(2)}) async-start(), calls=%async_computation.34 | async-start | bytes 2621440 | tf_op jit(solution)/shard_map/reduce_scatter | solution.py:29
  1313.4 183.1 %reduce-scatter.46.cloned.1.call-start = ((), (), s32[]{:S(2)}) async-start(), calls=%async_computation.42 | async-start | bytes 4718592 | tf_op jit(solution)/shard_map/reduce_scatter | solution.py:369
  1319.4 19.7 copy-start.31
  1319.4 26.6 copy-start.89
  1341.7 9.4 all-to-all-start.1
  1345.2 348.7 %reduce-scatter.64.cloned.1.call-start = ((), (), s32[]{:S(2)}) async-start(), calls=%async_computation.51 | async-start | bytes 2359296
  1446.8 403.9 %reduce-scatter.70.cloned.1.call-start = ((), (), s32[]{:S(2)}) async-start(), calls=%async_computation.54 | async-start | bytes 589824
  1452.0 399.7 %reduce-scatter.54.cloned.1.call-start = ((), (), s32[]{:S(2)}) async-start(), calls=%async_computation.46 | async-start | bytes 2359296 | tf_op jit(solution)/shard_map/reduce_scatter | solution.py:373
  1453.8 399.6 %reduce-scatter.48.cloned.1.call-start = ((), (), s32[]{:S(2)}) async-start(), calls=%async_computation.43 | async-start | bytes 2359296 | tf_op jit(solution)/shard_map/reduce_scatter | solution.py:370
  1462.3 32.0 copy-start.17
  1462.3 32.0 copy-start.19
  1462.3 32.0 copy-start.37
  1496.5 358.7 %reduce-scatter.68.cloned.1.call-start = ((), (), s32[]{:S(2)}) async-start(), calls=%async_computation.53 | async-start | bytes 589824
  1518.4 13.0 copy-start.70
  1518.5 13.0 copy-start.78
  1518.5 13.0 copy-start.80
  1531.0 340.7 %reduce-scatter.62.cloned.1.call-start = ((), (), s32[]{:S(2)}) async-start(), calls=%async_computation.50 | async-start | bytes 294912
  1668.7 237.7 %all-reduce.6.cloned.1.call-start = ((), (), s32[]{:S(2)}) async-start(), calls=%async_computation.55 | async-start | bytes 1048576 | tf_op jit(solution)/shard_map/psum | solution.py:382
  1695.6 1393.2 %reduce-scatter.66.cloned.1.call-start = ((), (), s32[]{:S(2)}) async-start(), calls=%async_computation.52 | async-start | bytes 84934656
  1826.5 1329.6 %reduce-scatter.56.cloned.1.call-start = ((), (), s32[]{:S(2)}) async-start(), calls=%async_computation.47 | async-start | bytes 1179648 | tf_op jit(solution)/shard_map/reduce_scatter | solution.py:374
  1829.2 1393.5 %reduce-scatter.52.cloned.1.call-start = ((), (), s32[]{:S(2)}) async-start(), calls=%async_computation.45 | async-start | bytes 1179648 | tf_op jit(solution)/shard_map/reduce_scatter | solution.py:372
  1830.7 1483.7 %reduce-scatter.60.cloned.1.call-start = ((), (), s32[]{:S(2)}) async-start(), calls=%async_computation.49 | async-start | bytes 4718592 | tf_op jit(solution)/shard_map/reduce_scatter | solution.py:376
  1836.0 1571.0 %reduce-scatter.58.cloned.1.call-start = ((), (), s32[]{:S(2)}) async-start(), calls=%async_computation.48 | async-start | bytes 4718592 | tf_op jit(solution)/shard_map/reduce_scatter | solution.py:375
  1840.8 1633.6 %reduce-scatter.50.cloned.1.call-start = ((), (), s32[]{:S(2)}) async-start(), calls=%async_computation.44 | async-start | bytes 1179648 | tf_op jit(solution)/shard_map/reduce_scatter | solution.py:371
  1843.6 1654.7 %reduce-scatter.44.cloned.1.call-start = ((), (), s32[]{:S(2)}) async-start(), calls=%async_computation.41 | async-start | bytes 655360 | tf_op jit(solution)/shard_map/reduce_scatter | solution.py:29
  3095.5 402.8 %copy-start.1 = (bf16[2,512]{1,0:T(2,128)(2,1)S(1)}, bf16[2,512]{1,0:T(2,128)(2,1)}, u32[]{:S(2)}) copy-start(bf16[2,512]{1,0:T(2,128)(2,1)} %param.40) | copy-start | bytes 6148
  (70 other events, 179.5 us)
Sparse Core Ops, SparseCore 0:
  10.2 42.9 all-gather.14
  55.3 715.1 all-gather.16
  773.1 39.4 all-gather.20
  819.4 15.7 all-gather.18
  855.0 28.4 reduce-scatter.31
  885.7 58.4 all-gather.22
  946.6 40.7 all-gather.24
  989.6 15.4 all-gather.26
  1009.8 31.3 reduce-scatter.33
  1043.3 49.3 all-gather.30
  1094.8 15.1 all-gather.28
  1112.0 16.7 all-gather.34
  1130.8 51.0 all-gather.32
  1190.7 29.5 reduce-scatter.37
  1222.7 16.7 all-gather.36
  1245.4 31.4 reduce-scatter.39
  1279.1 16.7 all-gather.38
  1307.6 31.4 reduce-scatter.41
  1341.8 31.4 reduce-scatter.35
  1376.7 87.8 reduce-scatter.45
  1468.6 67.2 reduce-scatter.63
  1539.7 61.0 reduce-scatter.69
  1604.3 67.3 reduce-scatter.53
  1675.1 67.3 reduce-scatter.47
  1746.4 60.9 reduce-scatter.67
  1811.5 60.1 reduce-scatter.61
  1874.1 32.2 all-reduce.5
  1910.8 1178.0 reduce-scatter.65
  3092.9 63.1 reduce-scatter.55
  3160.3 62.3 reduce-scatter.51
  3226.9 87.4 reduce-scatter.59
  3319.1 87.8 reduce-scatter.57
  3410.7 63.5 reduce-scatter.49
  3477.6 20.6 reduce-scatter.43
where the time goes:
time: 3510 us
  waiting for transfers between devices  2600 us (74%)
  local copies, waits for them, and re-layouts  369 us (11%)
  blocking collectives  230 us (7%)
  matrix products  210 us (6%)
  other arithmetic  70.8 us (2%)
    unnamed x39, waiting for transfers between devices  1200 us
    all_gather x1, waiting for transfers between devices, on_device(): lax.all_gather(kernel_bank, 'dp', axis=2, tiled=True)  642 us
    unnamed x224, local copies, waits for them, and re-layouts  276 us
    reduce_scatter x7, waiting for transfers between devices, scatter_rows(): lax.psum_scatter(partial_sum, 'head', scatter_dimension=1, tiled=True)  162 us
    reduce_scatter x1, waiting for transfers between devices, on_device(): lax.psum_scatter(mlp_in_grad, 'dp', scatter_dimension=0, tiled=True)  92.5 us
    reduce_scatter x1, waiting for transfers between devices, on_device(): lax.psum_scatter(mlp_out_grad, 'dp', scatter_dimension=1, tiled=True)  91.7 us
    all_gather x6, waiting for transfers between devices, gather_rows(): return lax.all_gather(piece, 'head', axis=1, tiled=True)  81.3 us
    all_gather x1, blocking collectives, on_device(): lax.all_gather(w_select, 'dp', axis=0, tiled=True)  73.6 us
  transfers between devices with their start and end apart: 35, of which 24 were waited for; matrix products, arithmetic and copies ran while one was open for 17% of the time, Pallas kernels for 0%

commit v1 on v0

v1 whole, which is shorter than its diff:
```python
from functools import partial

import jax
import jax.numpy as jnp
from jax import lax
from jax.experimental import pallas as pl
from jax.experimental.pallas import tpu as pltpu
from jax.sharding import PartitionSpec as P

DH = 64
CH = 16
RES = 16
HALF = RES // 2
LOW = HALF * HALF
PIX = RES * RES
EXTRA = 16
HIGH = lax.Precision.HIGHEST
ROOT_TWO = 1.4142135623730951
SLOPE = 0.2
DEMOD_EPS = 1e-08
BF = jnp.bfloat16
F32 = jnp.float32


def dot32(spec, *args):
    return jnp.einsum(spec, *args, preferred_element_type=F32)


def split_heads(array):
    return array.reshape(array.shape[:-1] + (array.shape[-1] // DH, DH))


def join_heads(array):
    return array.reshape(array.shape[:-2] + (array.shape[-2] * array.shape[-1],))


def hi_lo(value):
    high = value.astype(BF)
    return high, (value - high.astype(F32)).astype(BF)


def mix_body(blocks, mix_ref, bank_ref, mod2_ref, kern_ref, sums_ref):
    count = kern_ref.shape[0]
    wide = kern_ref.shape[3]

    @pl.when(pl.program_id(0) == 0)
    def _():
        sums_ref[...] = jnp.zeros_like(sums_ref)

    total = jnp.zeros((count, wide), F32)
    for block in range(blocks):
        rows = slice(block * CH, (block + 1) * CH)
        part = bank_ref[:, 0, rows, :].reshape(-1, wide)
        low = jnp.dot(mix_ref[...], part, preferred_element_type=F32).astype(BF)
        kern_ref[:, 0, rows, :] = low.reshape(count, CH, wide)
        full = low.astype(F32)
        square = full * full * mod2_ref[block]
        total = total + jnp.sum(square.reshape(count, CH, wide), axis=1)
    sums_ref[...] += total


def mix_kernels(mix_wide, bank, mod2_cols):
    kinds, taps, deep, wide = bank.shape
    count = mix_wide.shape[0] // CH
    return pl.pallas_call(
        partial(mix_body, deep // CH),
        grid=(taps,),
        in_specs=[
            pl.BlockSpec(mix_wide.shape, lambda t: (0, 0)),
            pl.BlockSpec((kinds, 1, deep, wide), lambda t: (0, t, 0, 0)),
            pl.BlockSpec(mod2_cols.shape, lambda t: (0, 0, 0)),
        ],
        out_specs=[
            pl.BlockSpec((count, 1, deep, wide), lambda t: (0, t, 0, 0)),
            pl.BlockSpec((count, wide), lambda t: (0, 0)),
        ],
        out_shape=[
            jax.ShapeDtypeStruct((count, taps, deep, wide), BF),
            jax.ShapeDtypeStruct((count, wide), F32),
        ],
        compiler_params=pltpu.CompilerParams(vmem_limit_bytes=48 << 20),
        name="mix_kernels",
    )(mix_wide, bank, mod2_cols)


def conv_body(win_ref, kern_ref, sums_ref, out_ref):
    deep = win_ref.shape[4]
    wide = kern_ref.shape[3]

    def window(tap):
        row_off, col_off = tap // 3, tap % 3
        rows = [win_ref[0, col_off, (y + row_off - 1) // 2 + 1] for y in range(RES)]
        return jnp.concatenate(rows, axis=0)

    if deep % 128 == 0:
        wins = jnp.concatenate([window(tap) for tap in range(9)], axis=1)
        total = jnp.dot(wins, kern_ref[0].reshape(9 * deep, wide), preferred_element_type=F32)
    else:
        total = jnp.zeros((PIX, wide), F32)
        for tap in range(9):
            total = total + jnp.dot(window(tap), kern_ref[0, tap], preferred_element_type=F32)
    out_ref[0, :PIX] = total.astype(BF)
    high = sums_ref[0].astype(BF).astype(F32)
    low = sums_ref[0] - high
    row = lax.broadcasted_iota(jnp.int32, (EXTRA, wide), 0)
    out_ref[0, PIX:] = jnp.where(row == 0, high, jnp.where(row == 1, low, 0.0)).astype(BF)


def conv_forward(windows, kernels, sums):
    count, taps, deep, wide = kernels.shape
    return pl.pallas_call(
        conv_body,
        grid=(count,),
        in_specs=[
            pl.BlockSpec((1,) + windows.shape[1:], lambda s: (s, 0, 0, 0, 0)),
            pl.BlockSpec((1, taps, deep, wide), lambda s: (s, 0, 0, 0)),
            pl.BlockSpec((1, 1, wide), lambda s: (s, 0, 0)),
        ],
        out_specs=pl.BlockSpec((1, PIX + EXTRA, wide), lambda s: (s, 0, 0)),
        out_shape=jax.ShapeDtypeStruct((count, PIX + EXTRA, wide), BF),
        compiler_params=pltpu.CompilerParams(vmem_limit_bytes=48 << 20),
        name="conv_forward",
    )(windows, kernels, sums[:, None, :])


def conv_back_body(
    order_ref, dconv_ref, kern_ref, turned_ref, mod2_ref, mod_ref, feat_ref, dkern_ref, dgrid_ref, dmod_ref
):
    deep, wide = kern_ref.shape[2], kern_ref.shape[3]
    grads = dconv_ref[0, 0, :PIX].astype(F32).reshape(RES, 2, HALF, wide)
    dsq = dconv_ref[0, 0, PIX:].astype(F32)
    dsq = jnp.sum(dsq, axis=0, keepdims=True)
    even, odd = grads[:, 0], grads[:, 1]
    none = jnp.zeros((RES, 1, wide), F32)
    after = jnp.concatenate([even[:, 1:], none], axis=1)
    before = jnp.concatenate([none, odd[:, :-1]], axis=1)
    by_col = (odd + after, even + odd, before + even)
    gap = jnp.zeros((1, HALF, wide), F32)
    into = jnp.zeros((2 * LOW, deep), F32)
    squares = jnp.zeros((deep, wide), F32)
    scaled = 2.0 * mod2_ref[0] * dsq
    for col_off in range(3):
        rows = by_col[col_off].reshape(HALF, 2, HALF, wide)
        first, second = rows[:, 0], rows[:, 1]
        by_row = (
            second + jnp.concatenate([first[1:], gap], axis=0),
            first + second,
            jnp.concatenate([gap, second[:-1]], axis=0) + first,
        )
        for row_off in range(3):
            tap = 3 * row_off + col_off
            exact = by_row[row_off].reshape(LOW, wide)
            high = exact.astype(BF)
            low = (exact - high.astype(F32)).astype(BF)
            both = jnp.concatenate([high, low], axis=0)
            kern = kern_ref[0, tap]
            full = kern.astype(F32)
            grad = jnp.dot(turned_ref[0], both, preferred_element_type=F32)
            dkern_ref[0, tap] = (grad + full * scaled).astype(BF)
            squares = squares + full * full
            into = into + lax.dot_general(
                both, kern, (((1,), (1,)), ((), ())), preferred_element_type=F32
            )
    dlow = into[:LOW] + into[LOW:]
    dgrid_ref[0] = dlow * mod_ref[0]
    direct = jnp.sum(dlow * feat_ref[0].astype(F32), axis=0, keepdims=True)
    through = lax.dot_general(
        jnp.broadcast_to(dsq, (8, wide)),
        squares,
        (((1,), (1,)), ((), ())),
        precision=HIGH,
        preferred_element_type=F32,
    )
    dmod_ref[0] = direct + 2.0 * mod_ref[0] * through[:1]


def conv_backward(order, dconv, kernels, turned, mod2_col, modulate, feats):
    count, taps, deep, wide = kernels.shape
    slots = dconv.shape[1]
    grid_spec = pltpu.PrefetchScalarGridSpec(
        num_scalar_prefetch=1,
        grid=(count,),
        in_specs=[
            pl.BlockSpec((1, 1, PIX + EXTRA, wide), lambda s, o: (o[s // slots], s % slots, 0, 0)),
            pl.BlockSpec((1, taps, deep, wide), lambda s, o: (s, 0, 0, 0)),
            pl.BlockSpec((1, deep, 2 * LOW), lambda s, o: (s, 0, 0)),
            pl.BlockSpec((1, deep, 1), lambda s, o: (s, 0, 0)),
            pl.BlockSpec((1, 1, deep), lambda s, o: (s, 0, 0)),
            pl.BlockSpec((1, LOW, deep), lambda s, o: (s, 0, 0)),
        ],
        out_specs=[
            pl.BlockSpec((1, taps, deep, wide), lambda s, o: (s, 0, 0, 0)),
            pl.BlockSpec((1, LOW, deep), lambda s, o: (s, 0, 0)),
            pl.BlockSpec((1, 1, deep), lambda s, o: (s, 0, 0)),
        ],
    )
    return pl.pallas_call(
        conv_back_body,
        grid_spec=grid_spec,
        out_shape=[
            jax.ShapeDtypeStruct((count, taps, deep, wide), BF),
            jax.ShapeDtypeStruct((count, LOW, deep), F32),
            jax.ShapeDtypeStruct((count, 1, deep), F32),
        ],
        compiler_params=pltpu.CompilerParams(vmem_limit_bytes=48 << 20),
        name="conv_backward",
    )(order, dconv, kernels, turned, mod2_col, modulate, feats)


def bank_back_body(blocks, mix_ref, dkern_ref, bank_ref, gbank_ref, cross_ref):
    wide = bank_ref.shape[3]

    @pl.when(pl.program_id(0) == 0)
    def _():
        cross_ref[...] = jnp.zeros_like(cross_ref)

    total = jnp.zeros(cross_ref.shape, F32)
    for block in range(blocks):
        rows = slice(block * CH, (block + 1) * CH)
        grads = dkern_ref[:, 0, rows, :].reshape(-1, wide)
        part = bank_ref[:, 0, rows, :].reshape(-1, wide)
        out = jnp.dot(mix_ref[...], grads, preferred_element_type=F32)
        gbank_ref[:, 0, rows, :] = out.reshape(-1, CH, wide)
        total = total + lax.dot_general(
            grads, part, (((1,), (1,)), ((), ())), preferred_element_type=F32
        )
    cross_ref[...] += total


def bank_backward(mix_wide_t, dkernels, bank):
    kinds, taps, deep, wide = bank.shape
    count = dkernels.shape[0]
    return pl.pallas_call(
        partial(bank_back_body, deep // CH),
        grid=(taps,),
        in_specs=[
            pl.BlockSpec(mix_wide_t.shape, lambda t: (0, 0)),
            pl.BlockSpec((count, 1, deep, wide), lambda t: (0, t, 0, 0)),
            pl.BlockSpec((kinds, 1, deep, wide), lambda t: (0, t, 0, 0)),
        ],
        out_specs=[
            pl.BlockSpec((kinds, 1, deep, wide), lambda t: (0, t, 0, 0)),
            pl.BlockSpec((count * CH, kinds * CH), lambda t: (0, 0)),
        ],
        out_shape=[
            jax.ShapeDtypeStruct(bank.shape, F32),
            jax.ShapeDtypeStruct((count * CH, kinds * CH), F32),
        ],
        compiler_params=pltpu.CompilerParams(vmem_limit_bytes=48 << 20),
        name="bank_backward",
    )(mix_wide_t, dkernels, bank)


class Exchange:
    def __init__(self, n_dp, n_h):
        self.n_dp, self.n_h = n_dp, n_h
        self.dp, self.head = lax.axis_index("dp"), lax.axis_index("head")

    def hop_head(self, x, step):
        return lax.ppermute(x, "head", [(i, i ^ step) for i in range(self.n_h)])

    def hop_dp(self, x, step):
        return lax.ppermute(x, "dp", [(i, i ^ step) for i in range(self.n_dp)])

    def gather_head(self, x):
        far = self.hop_head(x, 2)
        near = self.hop_head(x, 1)
        return [x, near, far, self.hop_head(far, 1)]

    def in_order(self, pieces):
        bit = (self.head & 1) == 1
        p, q, s, t = pieces
        p, q, s, t = (
            jnp.where(bit, q, p),
            jnp.where(bit, p, q),
            jnp.where(bit, t, s),
            jnp.where(bit, s, t),
        )
        bit = (self.head & 2) == 2
        return [
            jnp.where(bit, s, p),
            jnp.where(bit, t, q),
            jnp.where(bit, p, s),
            jnp.where(bit, q, t),
        ]

    def reduce_head(self, parts):
        send = jnp.stack([parts[1].astype(BF), parts[3].astype(BF)])
        got = self.hop_head(send, 1).astype(F32)
        other = self.hop_head((parts[2] + got[1]).astype(BF), 2)
        return parts[0] + got[0] + other.astype(F32)

    def reduce_dp(self, parts):
        if self.n_dp != 8:
            got = lax.all_to_all(parts, "dp", 0, 0, tiled=True)
            return jnp.sum(got.astype(F32), axis=0)
        y, z = self.dp & 1, self.dp >> 1
        pairs = parts.reshape((4, 2) + parts.shape[1:])
        keep = lax.dynamic_index_in_dim(pairs, y, 1, keepdims=False)
        send = lax.dynamic_index_in_dim(pairs, 1 - y, 1, keepdims=False)
        total = keep.astype(F32) + self.hop_dp(send, 1).astype(F32)
        out = lax.dynamic_index_in_dim(total, z, 0, keepdims=False)
        low = total.astype(BF)
        for step in (1, 2, 3):
            piece = lax.dynamic_index_in_dim(low, z ^ step, 0, keepdims=False)
            out = out + self.hop_dp(piece, 2 * step).astype(F32)
        return out

    def gather_dp(self, x):
        if self.n_dp != 8:
            return lax.all_gather(x, "dp", axis=0)
        return jnp.stack([x] + [self.hop_dp(x, k) for k in range(1, 8)])

    def order_dp(self):
        ranks = jnp.arange(self.n_dp, dtype=jnp.int32)
        return ranks ^ self.dp.astype(jnp.int32) if self.n_dp == 8 else ranks


def log_norm(scores):
    highest = jnp.max(scores, axis=-1, keepdims=True)
    return highest + jnp.log(jnp.sum(jnp.exp(scores - highest), axis=-1, keepdims=True))


def softmax_back(probs_full, dprobs):
    return probs_full * (dprobs - jnp.sum(probs_full * dprobs, axis=-1, keepdims=True))


def l2_scores(queries, keyset, score_scale):
    products = dot32("sphd,sqhd->shpq", queries, keyset)
    key_square = jnp.sum(jnp.square(keyset.astype(F32)), axis=-1)
    return (2.0 * products - jnp.transpose(key_square, (0, 2, 1))[:, :, None, :]) * score_scale


def on_device(
    n_dp,
    n_h,
    features,
    style_code,
    labels,
    counts,
    context,
    noise_map,
    w_select,
    w_mod,
    kernel_bank,
    conv_vecs,
    class_table,
    w_qkv,
    w_attn_out,
    w_cross_q,
    w_cross_kv,
    w_cross_out,
    w_mlp_in,
    w_mlp_out,
    w_rgb,
    cot_feat,
    cot_rgb,
):
    ex = Exchange(n_dp, n_h)
    slots, own_low, wide_all = features.shape
    kinds, taps, deep, wide = kernel_bank.shape
    own_pix = cot_feat.shape[1]
    count = n_dp * slots
    style_rows = w_select.shape[0]
    style_width = style_code.shape[1]
    hidden_own = w_mlp_in.shape[1]
    score_scale = DH ** (-0.5)

    label_parts = jnp.stack([labels // 256, labels % 256]).astype(BF)
    small = jnp.concatenate(
        [
            style_code.reshape(-1),
            w_select.reshape(-1),
            conv_vecs.reshape(-1),
            w_rgb.reshape(-1),
            label_parts.reshape(-1),
        ]
    )
    small_all = lax.all_gather(small, "dp", axis=0)
    sizes = [style_code.size, w_select.size, conv_vecs.size, w_rgb.size, label_parts.size]
    pieces, at = [], 0
    for size in sizes:
        pieces.append(small_all[:, at : at + size])
        at += size
    style_all = pieces[0].reshape(count, style_width)
    select_full = pieces[1].reshape(style_width, kinds)
    vecs_full = pieces[2].reshape(n_dp, 2, deep).transpose(1, 0, 2).reshape(2, wide_all)
    rgb_full = pieces[3].reshape(n_dp, 3, deep).transpose(1, 0, 2).reshape(3, wide_all)
    labels_all = pieces[4].reshape(n_dp, 2, slots).astype(jnp.int32)
    labels_all = (labels_all[:, 0] * 256 + labels_all[:, 1]).reshape(count)

    feats = lax.all_to_all(features, "dp", 2, 0, tiled=True)
    feats = lax.all_gather(feats, "head", axis=1, tiled=True)
    mod_cols = lax.all_to_all(w_mod, "dp", 1, 0, tiled=True)

    first = jnp.concatenate(
        [
            w_qkv.reshape(-1, wide),
            w_cross_kv.reshape(-1, wide),
            w_cross_q,
        ],
        axis=0,
    )
    second = jnp.concatenate([w_attn_out, w_cross_out], axis=1)
    first_all = lax.all_gather(first, "dp", axis=0)
    second_all = lax.all_gather(second, "dp", axis=0)
    mlp_pack = jnp.concatenate([w_mlp_in, w_mlp_out.T], axis=0)
    mlp_all = lax.all_gather(mlp_pack, "dp", axis=0)

    qkv_full = first_all[:, : 2 * deep].reshape(n_dp, 2, deep, wide).transpose(1, 0, 2, 3).reshape(2, wide_all, wide)
    cross_kv_full = first_all[:, 2 * deep : 4 * deep].reshape(n_dp, 2, deep, wide).transpose(1, 0, 2, 3).reshape(2, wide_all, wide)
    cross_q_own = first_all[:, 4 * deep :].reshape(wide_all, wide)
    attn_own = second_all[:, :, :deep].transpose(1, 0, 2).reshape(wide, wide_all)
    cross_out_own = second_all[:, :, deep:].transpose(1, 0, 2).reshape(wide, wide_all)
    mlp_in_own = mlp_all[:, :deep].reshape(wide_all, hidden_own)
    mlp_out_own_t = mlp_all[:, deep:].reshape(wide_all, hidden_own)
    attn_full = jnp.concatenate(ex.in_order(ex.gather_head(attn_own)), axis=0)
    cross_out_full = jnp.concatenate(ex.in_order(ex.gather_head(cross_out_own)), axis=0)
    cross_q_full = jnp.concatenate(ex.in_order(ex.gather_head(cross_q_own)), axis=1)

    mixing = jax.nn.softmax(jnp.dot(style_all, select_full, preferred_element_type=F32), axis=-1)
    mixing_low = mixing.astype(BF)
    unit = jnp.eye(CH, dtype=BF)
    mix_wide = (mixing_low[:, None, :, None] * unit[None, :, None, :]).reshape(count * CH, kinds * CH)
    modulate = 1.0 + jnp.dot(style_all, mod_cols, preferred_element_type=F32)
    mod2 = jnp.square(modulate)
    mod2_cols = mod2.reshape(count, deep // CH, CH).transpose(1, 0, 2).reshape(deep // CH, count * CH, 1)
    kernels, square_part = mix_kernels(mix_wide, kernel_bank, mod2_cols)
    mod_low = (feats.astype(F32) * modulate[:, None, :]).astype(BF)
    grid = jnp.repeat(mod_low.reshape(count, HALF, HALF, deep), 2, axis=2)
    grid = jnp.pad(grid, ((0, 0), (1, 1), (1, 1), (0, 0)))
    windows = jnp.stack([grid[:, :, b : b + RES] for b in range(3)], axis=1)
    conv_part = conv_forward(windows, kernels, square_part)
    conv_got = lax.all_to_all(
        conv_part.reshape(n_dp, slots, PIX + EXTRA, wide), "dp", 0, 0, tiled=True
    )
    conv_sum = jnp.sum(conv_got.astype(F32), axis=0)
    conv_raw = conv_sum[:, :PIX]
    demodulate = lax.rsqrt(conv_sum[:, PIX] + conv_sum[:, PIX + 1] + DEMOD_EPS)

    vecs_own = lax.dynamic_slice_in_dim(vecs_full, ex.head * wide, wide, 1).astype(F32)
    noise_full = noise_map.astype(F32)
    pre_act = conv_raw * demodulate[:, None, :] + vecs_own[0] * noise_full[:, :, None] + vecs_own[1]
    stream_cols = jnp.where(pre_act > 0, pre_act, SLOPE * pre_act) * ROOT_TWO
    cols_high, cols_low = hi_lo(stream_cols)
    full0 = jnp.concatenate(ex.in_order(ex.gather_head(cols_high)), axis=2)
    own_start = ex.head * own_pix
    stream0 = lax.dynamic_slice_in_dim(full0, own_start, own_pix, 1).astype(F32) + lax.all_to_all(
        cols_low, "head", 1, 2, tiled=True
    ).astype(F32)

    qkv_own = dot32("spi,nio->nspo", full0, qkv_full).astype(BF)
    queries, values_all = split_heads(qkv_own[0]), split_heads(qkv_own[1])
    scores = l2_scores(queries, queries, score_scale)
    self_norm = log_norm(scores)
    probs_low = jnp.exp(scores - self_norm).astype(BF)
    attended = join_heads(dot32("shpq,sqhd->sphd", probs_low, values_all).astype(BF))
    attended_pix = lax.all_to_all(attended, "head", 1, 2, tiled=True)
    stream1 = stream0 + dot32("spc,cd->spd", attended_pix, attn_full)
    low1 = stream1.astype(BF)

    table_rows = class_table.shape[0]
    one_hot = (
        labels_all[:, None] == ex.dp * table_rows + jnp.arange(table_rows, dtype=jnp.int32)[None, :]
    )
    class_part = jnp.dot(one_hot.astype(BF), class_table, preferred_element_type=F32).astype(BF)
    class_got = lax.all_to_all(class_part.reshape(n_dp, slots, wide_all), "dp", 0, 0, tiled=True)
    class_rows = jnp.sum(class_got.astype(F32), axis=0)
    tokens = (context.astype(F32) + class_rows[:, None, :]).astype(BF)
    cross_kv_own = dot32("sci,nio->nsco", tokens, cross_kv_full).astype(BF)
    cross_kv_heads = lax.all_gather(cross_kv_own, "head", axis=3, tiled=True)
    ckeys, cvalues = split_heads(cross_kv_heads[0]), split_heads(cross_kv_heads[1])

    cqueries = split_heads(dot32("spi,io->spo", low1, cross_q_full).astype(BF))
    cscores = dot32("sphd,schd->shpc", cqueries, ckeys) * score_scale
    cross_norm = log_norm(cscores)
    cprobs_full = jnp.exp(cscores - cross_norm)
    cprobs_low = cprobs_full.astype(BF)
    cout = join_heads(dot32("shpc,schd->sphd", cprobs_low, cvalues).astype(BF))
    stream2 = stream1 + dot32("spc,cd->spd", cout, cross_out_full)

    full2 = jnp.stack(ex.gather_head(stream2.astype(BF)))
    hidden = dot32("kspi,if->kspf", full2, mlp_in_own)
    active = jax.nn.gelu(hidden, approximate=True).astype(BF)
    stream3 = stream2 + ex.reduce_head(dot32("kspf,df->kspd", active, mlp_out_own_t))

    live_slots = (jnp.arange(slots, dtype=jnp.int32) < counts[0]).astype(F32)
    factor = live_slots / counts[0].astype(F32)
    features_out = (stream3 * live_slots[:, None, None]).astype(BF)
    final_low = stream3.astype(BF)
    colour = dot32("spi,ci->scp", final_low, rgb_full)
    rgb_out = (colour * live_slots[:, None, None]).astype(BF)
    dcolour = cot_rgb.astype(F32) * factor[:, None, None]
    dstream = cot_feat.astype(F32) * factor[:, None, None] + jnp.einsum(
        "scp,ci->spi", dcolour, rgb_full.astype(F32), precision=HIGH
    )
    rgb_part = jnp.einsum("scp,spi->ci", dcolour, final_low.astype(F32), precision=HIGH)

    dbranch = jnp.stack(ex.gather_head(dstream.astype(BF)))
    dactive = dot32("kspd,df->kspf", dbranch, mlp_out_own_t)
    _, gelu_pull = jax.vjp(partial(jax.nn.gelu, approximate=True), hidden)
    dhidden = gelu_pull(dactive)[0].astype(BF)
    dstream = dstream + ex.reduce_head(dot32("kspf,if->kspi", dhidden, mlp_in_own))
    mlp_out_grad = dot32("kspf,kspnd->nfd", active, dbranch.reshape(dbranch.shape[:3] + (n_dp, deep)))
    mlp_in_grad = dot32("kspi,kspf->if", full2, dhidden).reshape(n_dp, deep, hidden_own)
    grad_mlp_out = ex.reduce_dp(mlp_out_grad.astype(BF))
    grad_mlp_in = ex.reduce_dp(mlp_in_grad.astype(BF))

    dcross = dstream.astype(BF)
    dcout = split_heads(dot32("spd,cd->spc", dcross, cross_out_full).astype(BF))
    dcprobs = dot32("sphd,schd->shpc", dcout, cvalues)
    dcvalues_part = dot32("shpc,sphd->schd", cprobs_low, dcout)
    dcscores = softmax_back(cprobs_full, dcprobs).astype(BF)
    dcqueries = join_heads((dot32("shpc,schd->sphd", dcscores, ckeys) * score_scale).astype(BF))
    dckeys_part = dot32("shpc,sphd->schd", dcscores, cqueries) * score_scale
    dstream = dstream + dot32("spo,io->spi", dcqueries, cross_q_full)
    dkv_part = jnp.stack([join_heads(dckeys_part), join_heads(dcvalues_part)])
    dkv_got = lax.all_to_all(dkv_part.reshape(dkv_part.shape[:-1] + (n_h, wide)), "head", 3, 0, tiled=False)
    dcross_kv = jnp.sum(dkv_got, axis=0).astype(BF)
    cross_kv_grad = dot32("sci,nsco->nio", tokens, dcross_kv)
    dtokens_sum = jnp.sum(dot32("nsco,nio->sci", dcross_kv, cross_kv_full), axis=1)
    swapped = lax.all_to_all(jnp.stack([dcqueries, cout]), "head", 3, 2, tiled=True)
    dcq_cols, cout_cols = swapped[0], swapped[1]
    full1 = lax.all_gather(low1, "head", axis=1, tiled=True)
    dcross_all = lax.all_gather(dcross, "head", axis=1, tiled=True)
    cross_q_grad = dot32("spi,spo->io", full1, dcq_cols)
    cross_out_grad = dot32("spc,spnd->ncd", cout_cols, dcross_all.reshape(slots, PIX, n_dp, deep))
    grad_cross_out = ex.reduce_dp(cross_out_grad.astype(BF))
    grad_cross_q = ex.reduce_dp(cross_q_grad.astype(BF).reshape(n_dp, deep, wide))
    grad_cross_kv = ex.reduce_dp(
        cross_kv_grad.astype(BF).reshape(2, n_dp, deep, wide).transpose(1, 0, 2, 3)
    )

    dattn = dstream.astype(BF)
    dattended = dot32("spd,cd->spc", dattn, attn_full).astype(BF)
    dattended = split_heads(lax.all_to_all(dattended, "head", 2, 1, tiled=True))
    dattn_all = lax.all_gather(dattn, "head", axis=1, tiled=True)
    attn_out_grad = dot32("spc,spnd->ncd", attended, dattn_all.reshape(slots, PIX, n_dp, deep))
    grad_attn_out = ex.reduce_dp(attn_out_grad.astype(BF))
    dstream_cols = lax.all_to_all(dattn, "head", 2, 1, tiled=True)
    probs_full = jnp.exp(scores - self_norm)
    dprobs = dot32("sphd,sqhd->shpq", dattended, values_all)
    dvalues = dot32("shpq,sphd->sqhd", probs_low, dattended).astype(BF)
    dscores = softmax_back(probs_full, dprobs).astype(BF)
    column_sums = jnp.transpose(jnp.sum(dscores.astype(F32), axis=2), (0, 2, 1))
    as_query = dot32("shpq,sqhd->sphd", dscores, queries)
    as_key = dot32("shpq,sphd->sqhd", dscores, queries)
    dshared = (
        (as_query + as_key - queries.astype(F32) * column_sums[..., None]) * (2.0 * score_scale)
    ).astype(BF)
    dqkv = jnp.stack((join_heads(dshared), join_heads(dvalues)), axis=0)
    qkv_blocks = qkv_full.reshape(2, n_h, wide, wide)
    parts = [
        dot32(
            "nspo,nio->spi",
            dqkv,
            lax.dynamic_index_in_dim(qkv_blocks, ex.head ^ k, 1, keepdims=False),
        )
        for k in range(n_h)
    ]
    dconv_out = dstream_cols.astype(F32) + ex.reduce_head(parts)
    qkv_grad = dot32("spi,nspo->nio", full0, dqkv).astype(BF)
    grad_qkv = ex.reduce_dp(qkv_grad.reshape(2, n_dp, deep, wide).transpose(1, 0, 2, 3))

    dpre = dconv_out * ROOT_TWO * jnp.where(pre_act > 0, 1.0, SLOPE)
    vecs_part = jnp.stack(
        [jnp.sum(dpre * noise_full[:, :, None], axis=(0, 1)), jnp.sum(dpre, axis=(0, 1))]
    )
    ddemod = jnp.sum(dpre * conv_raw, axis=1)
    dsquare = ddemod * -0.5 * demodulate * demodulate * demodulate
    dconv = (dpre * demodulate[:, None, :]).astype(BF)
    dconv = dconv.reshape(slots, RES, HALF, 2, wide).transpose(0, 1, 3, 2, 4).reshape(slots, PIX, wide)
    dsq_high, dsq_low = hi_lo(dsquare)
    extra = jnp.pad(jnp.stack([dsq_high, dsq_low], axis=1), ((0, 0), (0, EXTRA - 2), (0, 0)))
    dconv_all = ex.gather_dp(jnp.concatenate([dconv, extra], axis=1))
    turned = mod_low.transpose(0, 2, 1)
    turned = jnp.concatenate([turned, turned], axis=2)
    dkernels, dgrid, dmod = conv_backward(
        ex.order_dp(), dconv_all, kernels, turned, mod2[:, :, None], modulate[:, None, :], feats
    )
    grad_bank, cross = bank_backward(mix_wide.T, dkernels, kernel_bank)
    dmixing_part = jnp.einsum("saka->sk", cross.reshape(count, CH, kinds, CH))

    pieces_in = dgrid.reshape(n_dp, slots, n_h, own_low, deep).transpose(0, 2, 1, 3, 4)
    pieces_in = pieces_in.reshape(n_dp * n_h, slots * own_low * deep)
    got = lax.all_to_all(pieces_in, ("dp", "head"), 0, 0, tiled=True)
    grad_input = jnp.sum(got.reshape(n_dp, n_h, slots, own_low, deep), axis=1)
    grad_input = grad_input.transpose(1, 2, 0, 3).reshape(slots, own_low, wide_all)

    tail = jnp.concatenate([dmod[:, 0, :].reshape(-1), dmixing_part.reshape(-1)])
    tail = lax.all_gather(tail, ("dp", "head"), axis=0).reshape(n_dp, n_h, -1)
    dmodulate = jnp.sum(tail[:, :, : count * deep], axis=1).reshape(n_dp, count, deep)
    dmodulate = dmodulate.transpose(1, 0, 2).reshape(count, wide_all)
    dmixing = jnp.sum(tail[:, :, count * deep :], axis=(0, 1)).reshape(count, kinds)
    style_own = lax.dynamic_slice_in_dim(style_all, ex.dp * style_rows, style_rows, 1).astype(F32)
    grad_mod = jnp.einsum("sr,sc->rc", style_own, dmodulate, precision=HIGH)
    logit_grad = mixing * (dmixing - jnp.sum(mixing * dmixing, axis=-1, keepdims=True))
    grad_select = jnp.einsum("sr,sk->rk", style_own, logit_grad, precision=HIGH)

    early = jnp.concatenate([rgb_part.reshape(-1), dtokens_sum.reshape(-1), vecs_part.reshape(-1)])
    early = lax.all_gather(early, ("dp", "head"), axis=0).reshape(n_dp, n_h, -1)
    at = 3 * wide_all
    rgb_sum = jnp.sum(early[:, :, :at], axis=(0, 1)).reshape(3, wide_all)
    grad_rgb = lax.dynamic_slice_in_dim(rgb_sum, ex.dp * deep, deep, 1)
    dtok_all = jnp.sum(early[:, :, at : at + slots * wide_all], axis=1).reshape(count, wide_all)
    grad_table = jnp.einsum("sr,sc->rc", one_hot.astype(F32), dtok_all, precision=HIGH)
    vecs_sum = jnp.sum(early[:, :, at + slots * wide_all :], axis=0).reshape(n_h, 2, wide)
    vecs_sum = vecs_sum.transpose(1, 0, 2).reshape(2, wide_all)
    grad_vecs = lax.dynamic_slice_in_dim(vecs_sum, ex.dp * deep, deep, 1)

    return (
        features_out,
        rgb_out,
        grad_input,
        grad_select,
        grad_mod,
        grad_bank,
        grad_vecs,
        grad_table,
        grad_qkv,
        grad_attn_out,
        grad_cross_q,
        grad_cross_kv,
        grad_cross_out,
        grad_mlp_in,
        grad_mlp_out,
        grad_rgb,
    )


def solution(mesh):
    return jax.shard_map(
        partial(on_device, mesh.shape["dp"], mesh.shape["head"]),
        mesh=mesh,
        in_specs=(
            P("dp", "head", None),
            P("dp", None),
            P("dp"),
            P("dp"),
            P("dp", None, None),
            P("dp", None),
            P("dp", None),
            P("dp", None),
            P(None, None, "dp", "head"),
            P(None, "dp"),
            P("dp", None),
            P(None, "dp", "head"),
            P("head", "dp"),
            P("dp", "head"),
            P(None, "dp", "head"),
            P("head", "dp"),
            P("dp", "head"),
            P("head", "dp"),
            P(None, "dp"),
            P("dp", "head", None),
            P("dp", None, "head"),
        ),
        out_specs=(
            P("dp", "head", None),
            P("dp", None, "head"),
            P("dp", "head", None),
            P("dp", None),
            P("dp", None),
            P(None, None, "dp", "head"),
            P(None, "dp"),
            P("dp", None),
            P(None, "dp", "head"),
            P("head", "dp"),
            P("dp", "head"),
            P(None, "dp", "head"),
            P("head", "dp"),
            P("dp", "head"),
            P("head", "dp"),
            P(None, "dp"),
        ),
        check_vma=False,
    )
```

time: 3510 us -> 713 us (0.20)
  waiting for transfers between devices: 2600 us -> 113 us
  local copies, waits for them, and re-layouts: 369 us -> 127 us
  matrix products: 210 us -> 58.7 us
  starting transfers between devices: 6.21 us -> 125 us
  blocking collectives: 230 us -> 156 us
  Pallas kernels: 0 us -> 50.1 us
    unnamed x39 -> x6, waiting for transfers between devices: 1200 us -> 0.1 us
    all_gather x13 -> x6, waiting for transfers between devices: 839 us -> 0.03 us  [the longest x1 0.02 us: on_device(): dcross_all = lax.all_gather(dcross, 'head', axis=1, tiled=True)]
    reduce_scatter x15 -> x0, waiting for transfers between devices: 534 us -> none  [the longest x7 162 us: scatter_rows(): lax.psum_scatter(partial_sum, 'head', scatter_dimension=1, tiled=True)]
    unnamed x224 -> x288, local copies, waits for them, and re-layouts: 276 us -> 46.6 us
    dot_general x74 -> x45, matrix products: 210 us -> 58.7 us  [the longest x37 53.4 us: dot32(): return jnp.einsum(spec, *args, preferred_element_type=F32)]
    all_gather x7 -> x4, blocking collectives: 213 us -> 117 us  [the longest x1 53.4 us: on_device(): early = lax.all_gather(early, ('dp', 'head'), axis=0).reshape(n_dp, n_h, -1)]
    ppermute x0 -> x59, waiting for transfers between devices: none -> 74.1 us  [the longest x35 53.1 us: hop_dp(): return lax.ppermute(x, 'dp', [(i, i ^ step) for i in range(self.n_dp)])]
    ppermute x0 -> x59, starting transfers between devices: none -> 68 us  [the longest x35 54.3 us: hop_dp(): return lax.ppermute(x, 'dp', [(i, i ^ step) for i in range(self.n_dp)])]
  transfers between devices with their start and end apart: 35 -> 76, of which waited for: 24 -> 24; matrix products, arithmetic and copies ran while one was open for 17% -> 32% of each run, Pallas kernels for 0% -> 7%
where the time goes in v1:
time: 713 us; the launch traced here: 701 us
  blocking collectives  156 us (22%)
  local copies, waits for them, and re-layouts  127 us (18%)
  starting transfers between devices  125 us (18%)
  waiting for transfers between devices  113 us (16%)
  matrix products  58.7 us (8%)
  other arithmetic  52.7 us (7%)
  Pallas kernels  50.1 us (7%)
  between operations  18.5 us (3%)
    ppermute x35, starting transfers between devices, hop_dp(): return lax.ppermute(x, 'dp', [(i, i ^ step) for i in range(self.n_dp)])  54.3 us
    dot_general x37, matrix products, dot32(): return jnp.einsum(spec, *args, preferred_element_type=F32)  53.4 us
    all_gather x1, blocking collectives, on_device(): early = lax.all_gather(early, ('dp', 'head'), axis=0).reshape(n_dp, n_h, -1)  53.4 us
    ppermute x35, waiting for transfers between devices, hop_dp(): return lax.ppermute(x, 'dp', [(i, i ^ step) for i in range(self.n_dp)])  53.1 us
    unnamed x288, local copies, waits for them, and re-layouts  46.6 us
    all_gather x1, blocking collectives, on_device(): tail = lax.all_gather(tail, ('dp', 'head'), axis=0).reshape(n_dp, n_h, -1)  42.5 us
    unnamed x1, blocking collectives  38.2 us
    all_to_all x1, waiting for transfers between devices, on_device(): lax.all_to_all(conv_part.reshape(n_dp, slots, PIX + EXTRA, wide), 'dp', 0...  30.2 us
  transfers between devices with their start and end apart: 76, of which 24 were waited for; matrix products, arithmetic and copies ran while one was open for 32% of the time, Pallas kernels for 7%

profile of v1, /device:TPU:0, one launch (start us, length us, event | category | flops | bytes accessed | tf_op | source)
XLA Modules:
  0.0 700.7 jit_solution(10167567835936049580)
XLA Ops:
  11.3 7.3 %all-to-all-start = ((bf16[8,2,2048]{2,1,0:T(2,128)(2,1)}), bf16[8,2,2048]{2,1,0:T(2,128)(2,1)S(1)}, u32[]{:S(2)}, u32[]{:S(2)}) async-start(bf16[8,2,2048]{2,1,0:T(2,128)(2,1)} %reshape.486), calls=%async_computation | async-start | bytes 131072 | tf_op jit(solution)/shard_map/all_to_all | solution.py:392
  23.2 38.2 %all-reduce.2 = bf16[17440]{0:T(1024)(128)(2,1)S(1)} all-reduce(bf16[17440]{0:T(1024)(128)(2,1)S(1)} %dynamic-update-slice), channel_id=2, replica_groups=mesh['dp'=8,'head'=4] {'dp'}, use_global_device_ids=true, to_apply=%add.2 | all-reduce | flops 17440 | bytes 69760
  64.4 3.4 all-to-all-start.1
  69.3 5.8 all_gather.51.feat_ref
  76.8 4.2 all-to-all-start.5
  84.6 2.3 copy-done.2
  86.9 8.7 %mix_kernels.1 = (bf16[16,9,128,256]{3,2,1,0:T(8,128)(2,1)}, f32[16,256]{1,0:T(8,128)S(1)}) custom-call(bf16[256,128]{1,0:T(8,128)(2,1)S(1)} %copy.361.mix_ref, bf16[8,9,128,256]{3,2,1,0:T(8,128)(2,1)S(1)} %copy-done.2, f32[8,256,1]{2,1,0:T(8,128)S(1)} %reshape.481.mod2_ref), custom_call_target="tpu_custom_call" | custom-call | tf_op jit(solution)/shard_map/mix_kernels/pallas_call | solution.py:65
  95.6 13.2 %conv_forward.1 = bf16[16,272,256]{2,1,0:T(8,128)(2,1)} custom-call(bf16[16,3,10,16,128]{4,3,2,1,0:T(8,128)(2,1)S(1)} %pad_maximum_fusion.win_ref, bf16[16,9,128,256]{3,2,1,0:T(8,128)(2,1)} %get-tuple-element.23.kern_ref, f32[16,1,256]{2,1,0:T(1,128)S(1)} %broadcast_in_dim.17.sums_ref), custom_call_target="tpu_custom_call" | custom-call | tf_op jit(solution)/shard_map/conv_forward/pallas_call | solution.py:111
  108.8 6.1 all-to-all-start.2
  130.6 3.8 collective-permute-done.3
  135.1 4.9 collective-permute-done.18
  140.5 9.3 %collective-permute-done.9 = bf16[256,1024]{1,0:T(8,128)(2,1)} collective-permute-done((bf16[256,1024]{1,0:T(8,128)(2,1)}, bf16[256,1024]{1,0:T(8,128)(2,1)}, u32[]{:S(2)}, u32[]{:S(2)}) %collective-permute-start.9) | collective-permute-done | bytes 524320 | tf_op jit(solution)/shard_map/ppermute | solution.py:260
  149.8 2.9 broadcast_select_fusion.23
  152.7 30.2 %all-to-all-done.2 = bf16[8,2,272,256]{3,2,1,0:T(8,128)(2,1)S(1)} async-done(((bf16[8,2,272,256]{3,2,1,0:T(8,128)(2,1)}), bf16[8,2,272,256]{3,2,1,0:T(8,128)(2,1)S(1)}, u32[]{:S(2)}, u32[]{:S(2)}) %all-to-all-start.2) | async-done | bytes 2228256 | tf_op jit(solution)/shard_map/all_to_all | solution.py:434
  187.3 3.6 all-to-all-start.3
  191.0 3.0 broadcast_select_fusion.19
  194.4 2.5 all-to-all-done.3
  205.6 15.7 %all_gather.58 = bf16[2,2,16,1024]{3,2,1,0:T(8,128)(2,1)} all-gather(bf16[2,2,16,256]{3,2,1,0:T(8,128)(2,1)S(1)} %fusion.24), channel_id=1, replica_groups=mesh['dp'=8,'head'=4] {'head'}, dimensions={3}, use_global_device_ids=true | all-gather | bytes 163840 | tf_op jit(solution)/shard_map/all_gather | solution.py:471
  227.7 3.4 all-to-all-start.4
  234.2 2.9 all-to-all-done.4
  237.1 3.0 fusion.188
  240.2 2.9 broadcast_select_fusion.7
  247.2 2.5 fusion.190
  259.7 2.4 copy.425
  262.6 6.8 copy.468
  269.4 2.7 fusion.177
  272.2 2.5 fusion.100
  276.2 4.3 fusion.6
  295.3 3.0 collective-permute-done.21
  300.0 2.4 convolution_convert_fusion.4
  306.2 2.4 convolution_convert_fusion.3
  312.9 4.0 all-to-all-start.7
  332.8 2.8 fusion.194
  337.2 4.0 all-to-all-start.6
  349.5 4.0 all-to-all-start.9
  363.5 4.4 all-to-all-start.10
  372.0 5.4 constant_dynamic-slice_fusion.10
  377.4 3.5 copy.417
  380.9 3.5 copy.474
  384.3 3.5 copy.428
  391.5 3.5 fusion.168
  403.1 3.8 collective-permute-start.58
  412.9 2.3 copy.426
  419.1 7.0 collective-permute-start.53
  426.0 9.5 %collective-permute-done.57 = bf16[1024,128]{1,0:T(8,128)(2,1)} collective-permute-done((bf16[1024,128]{1,0:T(8,128)(2,1)}, bf16[1024,128]{1,0:T(8,128)(2,1)}, u32[]{:S(2)}, u32[]{:S(2)}) %collective-permute-start.57) | collective-permute-done | bytes 262176 | tf_op jit(solution)/shard_map/ppermute | solution.py:263
  441.0 5.4 collective-permute-done.52
  448.6 2.5 collective-permute-start.42
  458.4 7.4 %collective-permute-done.43 = bf16[4,2,128,256]{3,2,1,0:T(8,128)(2,1)S(1)} collective-permute-done((bf16[4,2,128,256]{3,2,1,0:T(8,128)(2,1)S(1)}, bf16[4,2,128,256]{3,2,1,0:T(8,128)(2,1)S(1)}, u32[]{:S(2)}, u32[]{:S(2)}) %collective-permute-start.43) | collective-permute-done | bytes 524320 | tf_op jit(solution)/shard_map/ppermute | solution.py:263
  465.8 2.4 collective-permute-start.34
  470.5 2.4 collective-permute-start.46
  474.1 8.8 %collective-permute-start.45 = (bf16[2,128,256]{2,1,0:T(8,128)(2,1)S(1)}, bf16[2,128,256]{2,1,0:T(8,128)(2,1)S(1)}, u32[]{:S(2)}, u32[]{:S(2)}) collective-permute-start(bf16[2,128,256]{2,1,0:T(8,128)(2,1)S(1)} %get-tuple-element.177), channel_id=1, source_target_pairs={{0,16},{4,20},{8,24},{12,28},{16,0},{20,4},{24,8},{28,12},{1,17},{... | collective-permute-start | bytes 393224 | tf_op jit(solution)/shard_map/ppermute | solution.py:263
  485.2 5.2 collective-permute-done.45
  493.7 3.3 collective-permute-start.26
  499.7 53.4 %all-gather.7 = f32[32,1,5632]{2,1,0:T(1,128)S(1)} all-gather(f32[1,1,5632]{2,1,0:T(1,128)S(1)} %reshape.445), channel_id=7, replica_groups=mesh['dp'=8,'head'=4] {'dp','head'}, dimensions={0}, use_global_device_ids=true | all-gather | bytes 743424 | tf_op jit(solution)/shard_map/all_gather | solution.py:601
  564.8 5.5 collective-permute-done.29
  570.3 2.7 collective-permute-done.30
  573.0 16.1 %conv_backward.1 = (bf16[16,9,128,256]{3,2,1,0:T(8,128)(2,1)}, f32[16,64,128]{2,1,0:T(8,128)S(1)}, f32[16,1,128]{2,1,0:T(1,128)S(1)}) custom-call(s32[8]{0:T(128)S(1)} %iota_xor_fusion.order_ref, bf16[8,2,272,256]{3,2,1,0:T(8,128)(2,1)S(1)} %bitcast_dynamic-update-slice_fusion.dconv_ref, bf16[16,9,128,256]{3,2,1,0:T(8,128)(2,1)} %get-tuple-element.23.kern_ref, ...), custom_call_target="tpu_custom_call" | custom-call | tf_op jit(solution)/shard_map/conv_backward/pallas_call | solution.py:197
  590.0 12.0 %all-to-all-start.8 = ((f32[32,1,4096]{2,1,0:T(1,128)}), f32[32,1,4096]{2,1,0:T(1,128)S(1)}, u32[]{:S(2)}, u32[]{:S(2)}) async-start(f32[32,1,4096]{2,1,0:T(1,128)} %bitcast.134), calls=%async_computation.8 | async-start | bytes 1048576 | tf_op jit(solution)/shard_map/all_to_all | solution.py:586
  604.4 12.1 %bank_backward.1 = (f32[8,9,128,256]{3,2,1,0:T(8,128)}, f32[256,128]{1,0:T(8,128)S(1)}) custom-call(bf16[128,256]{1,0:T(8,128)(2,1)S(1)} %bitcast.653, bf16[16,9,128,256]{3,2,1,0:T(8,128)(2,1)} %get-tuple-element.27.dkern_ref, bf16[8,9,128,256]{3,2,1,0:T(8,128)(2,1)S(1)} %copy-done.3), custom_call_target="tpu_custom_call" | custom-call | tf_op jit(solution)/shard_map/bank_backward/pallas_call | solution.py:233
  617.1 42.5 %all-gather.6 = f32[32,1,2176]{2,1,0:T(1,128)S(1)} all-gather(f32[1,1,2176]{2,1,0:T(1,128)S(1)} %reshape.443), channel_id=6, replica_groups=mesh['dp'=8,'head'=4] {'dp','head'}, dimensions={0}, use_global_device_ids=true | all-gather | bytes 287232 | tf_op jit(solution)/shard_map/all_gather | solution.py:591
  668.3 5.3 collective-permute-done.35
  673.8 4.9 collective-permute-done.47
  679.3 4.4 collective-permute-start.36
  685.8 3.0 collective-permute-start.48
  (638 shorter events, 215.5 us)
Async XLA Ops:
  7.3 108.6 %all-gather.23.cloned.1.call-start = ((), (), s32[]{:S(2)}) async-start(), calls=%async_computation.15 | async-start | bytes 1179648 | tf_op jit(solution)/shard_map/all_gather | solution.py:406
  11.3 53.0 %all-to-all-start = ((bf16[8,2,2048]{2,1,0:T(2,128)(2,1)}), bf16[8,2,2048]{2,1,0:T(2,128)(2,1)S(1)}, u32[]{:S(2)}, u32[]{:S(2)}) async-start(bf16[8,2,2048]{2,1,0:T(2,128)(2,1)} %reshape.486), calls=%async_computation | async-start | bytes 131072 | tf_op jit(solution)/shard_map/all_to_all | solution.py:392
  18.6 179.6 %all-gather.21.cloned.1.call-start = ((), (), s32[]{:S(2)}) async-start(), calls=%async_computation.14 | async-start | bytes 2949120 | tf_op jit(solution)/shard_map/all_gather | solution.py:405
  64.4 12.4 %all-to-all-start.1 = ((bf16[64,8,128]{2,0,1:T(8,128)(2,1)}), bf16[64,8,128]{2,0,1:T(8,128)(2,1)S(1)}, u32[]{:S(2)}, u32[]{:S(2)}) async-start(bf16[64,8,128]{2,0,1:T(8,128)(2,1)} %copy_bitcast_fusion.4), calls=%async_computation.1 | async-start | bytes 262144 | tf_op jit(solution)/shard_map/all_to_all | solution.py:394
  76.8 32.1 %all-to-all-start.5 = ((bf16[8,2,1024]{2,1,0:T(2,128)(2,1)}), bf16[8,2,1024]{2,1,0:T(2,128)(2,1)S(1)}, u32[]{:S(2)}, u32[]{:S(2)}) async-start(bf16[8,2,1024]{2,1,0:T(2,128)(2,1)} %reshape.380), calls=%async_computation.5 | async-start | bytes 65536 | tf_op jit(solution)/shard_map/all_to_all | solution.py:467
  108.8 74.0 %all-to-all-start.2 = ((bf16[8,2,272,256]{3,2,1,0:T(8,128)(2,1)}), bf16[8,2,272,256]{3,2,1,0:T(8,128)(2,1)S(1)}, u32[]{:S(2)}, u32[]{:S(2)}) async-start(bf16[8,2,272,256]{3,2,1,0:T(8,128)(2,1)} %bitcast.18), calls=%async_computation.2 | async-start | bytes 4456448 | tf_op jit(solution)/shard_map/all_to_all | solution.py:434
  115.0 147.6 %all-gather.25.cloned.1.call-start = ((), (), s32[]{:S(2)}) async-start(), calls=%async_computation.16 | async-start | bytes 4718592 | tf_op jit(solution)/shard_map/all_gather | solution.py:408
  119.2 15.2 %collective-permute-start.3 = (bf16[256,1024]{1,0:T(8,128)(2,1)}, bf16[256,1024]{1,0:T(8,128)(2,1)}, u32[]{:S(2)}, u32[]{:S(2)}) collective-permute-start(bf16[256,1024]{1,0:T(8,128)(2,1)} %bitcast.641), channel_id=1, source_target_pairs={{0,2},{1,3},{2,0},{3,1},{4,6},{5,7},{6,4},{7,5},{8,10},{9,11},{10,... | collective-permute-start | bytes 1572872 | tf_op jit(solution)/shard_map/ppermute | solution.py:260
  121.9 18.1 %collective-permute-start.18 = (bf16[2,64,1024]{2,1,0:T(8,128)(2,1)}, bf16[2,64,1024]{2,1,0:T(8,128)(2,1)}, u32[]{:S(2)}, u32[]{:S(2)}) collective-permute-start(bf16[2,64,1024]{2,1,0:T(8,128)(2,1)} %get-tuple-element.219), channel_id=1, source_target_pairs={{0,2},{1,3},{2,0},{3,1},{4,6},{5,7},{6,4},{7,5},{8,10},{9,11},{10,... | collective-permute-start | bytes 786440 | tf_op jit(solution)/shard_map/ppermute | solution.py:260
  122.6 132.5 %collective-permute-start.17 = (bf16[2,64,1024]{2,1,0:T(8,128)(2,1)}, bf16[2,64,1024]{2,1,0:T(8,128)(2,1)}, u32[]{:S(2)}, u32[]{:S(2)}) collective-permute-start(bf16[2,64,1024]{2,1,0:T(8,128)(2,1)} %get-tuple-element.219), channel_id=1, source_target_pairs={{0,1},{1,0},{2,3},{3,2},{4,5},{5,4},{6,7},{7,6},{8,9},{9,8},{10,11... | collective-permute-start | bytes 786440 | tf_op jit(solution)/shard_map/ppermute | solution.py:260
  125.6 14.4 %collective-permute-start.5 = (bf16[256,1024]{1,0:T(8,128)(2,1)}, bf16[256,1024]{1,0:T(8,128)(2,1)}, u32[]{:S(2)}, u32[]{:S(2)}) collective-permute-start(bf16[256,1024]{1,0:T(8,128)(2,1)} %bitcast.641), channel_id=1, source_target_pairs={{0,1},{1,0},{2,3},{3,2},{4,5},{5,4},{6,7},{7,6},{8,9},{9,8},{10,11... | collective-permute-start | bytes 1572872 | tf_op jit(solution)/shard_map/ppermute | solution.py:260
  129.2 20.5 %collective-permute-start.9 = (bf16[256,1024]{1,0:T(8,128)(2,1)}, bf16[256,1024]{1,0:T(8,128)(2,1)}, u32[]{:S(2)}, u32[]{:S(2)}) collective-permute-start(bf16[256,1024]{1,0:T(8,128)(2,1)} %bitcast.640), channel_id=1, source_target_pairs={{0,2},{1,3},{2,0},{3,1},{4,6},{5,7},{6,4},{7,5},{8,10},{9,11},{10,... | collective-permute-start | bytes 1572872 | tf_op jit(solution)/shard_map/ppermute | solution.py:260
  134.4 15.4 %collective-permute-start.4 = (bf16[256,1024]{1,0:T(8,128)(2,1)}, bf16[256,1024]{1,0:T(8,128)(2,1)}, u32[]{:S(2)}, u32[]{:S(2)}) collective-permute-start(bf16[256,1024]{1,0:T(8,128)(2,1)} %collective-permute-done.3), channel_id=1, source_target_pairs={{0,1},{1,0},{2,3},{3,2},{4,5},{5,4},{6,7},{7,6},{8,9},{9,8},{10,11... | collective-permute-start | bytes 1572872 | tf_op jit(solution)/shard_map/ppermute | solution.py:260
  140.0 116.8 %collective-permute-start.19 = (bf16[2,64,1024]{2,1,0:T(8,128)(2,1)}, bf16[2,64,1024]{2,1,0:T(8,128)(2,1)}, u32[]{:S(2)}, u32[]{:S(2)}) collective-permute-start(bf16[2,64,1024]{2,1,0:T(8,128)(2,1)} %collective-permute-done.18), channel_id=1, source_target_pairs={{0,1},{1,0},{2,3},{3,2},{4,5},{5,4},{6,7},{7,6},{8,9},{9,8},{10,11... | collective-permute-start | bytes 786440 | tf_op jit(solution)/shard_map/ppermute | solution.py:260
  140.0 50.9 %collective-permute-start.11 = (bf16[256,1024]{1,0:T(8,128)(2,1)}, bf16[256,1024]{1,0:T(8,128)(2,1)}, u32[]{:S(2)}, u32[]{:S(2)}) collective-permute-start(bf16[256,1024]{1,0:T(8,128)(2,1)} %bitcast.640), channel_id=1, source_target_pairs={{0,1},{1,0},{2,3},{3,2},{4,5},{5,4},{6,7},{7,6},{8,9},{9,8},{10,11... | collective-permute-start | bytes 1572872 | tf_op jit(solution)/shard_map/ppermute | solution.py:260
  149.8 41.2 %collective-permute-start.10 = (bf16[256,1024]{1,0:T(8,128)(2,1)}, bf16[256,1024]{1,0:T(8,128)(2,1)}, u32[]{:S(2)}, u32[]{:S(2)}) collective-permute-start(bf16[256,1024]{1,0:T(8,128)(2,1)} %collective-permute-done.9), channel_id=1, source_target_pairs={{0,1},{1,0},{2,3},{3,2},{4,5},{5,4},{6,7},{7,6},{8,9},{9,8},{10,11... | collective-permute-start | bytes 1572872 | tf_op jit(solution)/shard_map/ppermute | solution.py:260
  184.9 13.3 %collective-permute-start = (bf16[2,256,256]{2,1,0:T(8,128)(2,1)}, bf16[2,256,256]{2,1,0:T(8,128)(2,1)}, u32[]{:S(2)}, u32[]{:S(2)}) collective-permute-start(bf16[2,256,256]{2,1,0:T(8,128)(2,1)} %get-tuple-element.132), channel_id=1, source_target_pairs={{0,2},{1,3},{2,0},{3,1},{4,6},{5,7},{6,4},{7,5},{8,10},{9,11},{10,... | collective-permute-start | bytes 786440 | tf_op jit(solution)/shard_map/ppermute | solution.py:260
  187.3 9.6 %all-to-all-start.3 = ((bf16[2,256,256]{2,0,1:T(2,128)(2,1)}), bf16[2,256,256]{2,0,1:T(2,128)(2,1)S(1)}, u32[]{:S(2)}, u32[]{:S(2)}) async-start(bf16[2,256,256]{2,0,1:T(2,128)(2,1)} %copy.363), calls=%async_computation.3 | async-start | bytes 524288 | tf_op jit(solution)/shard_map/all_to_all | solution.py:448
  193.9 27.4 %collective-permute-start.2 = (bf16[2,256,256]{2,1,0:T(8,128)(2,1)}, bf16[2,256,256]{2,1,0:T(8,128)(2,1)}, u32[]{:S(2)}, u32[]{:S(2)}) collective-permute-start(bf16[2,256,256]{2,1,0:T(8,128)(2,1)} %get-tuple-element.132), channel_id=1, source_target_pairs={{0,1},{1,0},{2,3},{3,2},{4,5},{5,4},{6,7},{7,6},{8,9},{9,8},{10,11... | collective-permute-start | bytes 786440 | tf_op jit(solution)/shard_map/ppermute | solution.py:260
  198.2 23.5 %collective-permute-start.1 = (bf16[2,256,256]{2,1,0:T(8,128)(2,1)}, bf16[2,256,256]{2,1,0:T(8,128)(2,1)}, u32[]{:S(2)}, u32[]{:S(2)}) collective-permute-start(bf16[2,256,256]{2,1,0:T(8,128)(2,1)} %collective-permute-done), channel_id=1, source_target_pairs={{0,1},{1,0},{2,3},{3,2},{4,5},{5,4},{6,7},{7,6},{8,9},{9,8},{10,11... | collective-permute-start | bytes 786440 | tf_op jit(solution)/shard_map/ppermute | solution.py:260
  204.9 26.2 %collective-permute-start.6 = (bf16[1024,256]{1,0:T(8,128)(2,1)S(1)}, bf16[1024,256]{1,0:T(8,128)(2,1)}, u32[]{:S(2)}, u32[]{:S(2)}) collective-permute-start(bf16[1024,256]{1,0:T(8,128)(2,1)S(1)} %bitcast.683), channel_id=1, source_target_pairs={{0,2},{1,3},{2,0},{3,1},{4,6},{5,7},{6,4},{7,5},{8,10},{9,11},{10,... | collective-permute-start | bytes 1572872 | tf_op jit(solution)/shard_map/ppermute | solution.py:260
  221.3 18.9 %collective-permute-start.8 = (bf16[1024,256]{1,0:T(8,128)(2,1)S(1)}, bf16[1024,256]{1,0:T(8,128)(2,1)}, u32[]{:S(2)}, u32[]{:S(2)}) collective-permute-start(bf16[1024,256]{1,0:T(8,128)(2,1)S(1)} %bitcast.684), channel_id=1, source_target_pairs={{0,1},{1,0},{2,3},{3,2},{4,5},{5,4},{6,7},{7,6},{8,9},{9,8},{10,11... | collective-permute-start | bytes 1572872 | tf_op jit(solution)/shard_map/ppermute | solution.py:260
  231.1 186.1 %all-gather.17.cloned.1.call-start = ((), (), s32[]{:S(2)}) async-start(), calls=%async_computation.12 | async-start | bytes 1310720 | tf_op jit(solution)/shard_map/all_gather | solution.py:524
  249.7 12.4 %collective-permute-start.13 = (bf16[2,64,1024]{2,1,0:T(8,128)(2,1)}, bf16[2,64,1024]{2,1,0:T(8,128)(2,1)}, u32[]{:S(2)}, u32[]{:S(2)}) collective-permute-start(bf16[2,64,1024]{2,1,0:T(8,128)(2,1)} %get-tuple-element.215), channel_id=1, source_target_pairs={{0,2},{1,3},{2,0},{3,1},{4,6},{5,7},{6,4},{7,5},{8,10},{9,11},{10,... | collective-permute-start | bytes 786440 | tf_op jit(solution)/shard_map/ppermute | solution.py:260
  259.6 403.1 %all-gather.15.cloned.1.call-start = ((), (), s32[]{:S(2)}) async-start(), calls=%async_computation.11 | async-start | bytes 1310720 | tf_op jit(solution)/shard_map/all_gather | solution.py:537
  259.7 12.5 %collective-permute-start.12 = (bf16[2,64,1024]{2,1,0:T(8,128)(2,1)}, bf16[2,64,1024]{2,1,0:T(8,128)(2,1)S(1)}, u32[]{:S(2)}, u32[]{:S(2)}) collective-permute-start(bf16[2,64,1024]{2,1,0:T(8,128)(2,1)} %get-tuple-element.215), channel_id=1, source_target_pairs={{0,1},{1,0},{2,3},{3,2},{4,5},{5,4},{6,7},{7,6},{8,9},{9,8},{10,11... | collective-permute-start | bytes 786440 | tf_op jit(solution)/shard_map/ppermute | solution.py:260
  262.1 10.1 %collective-permute-start.14 = (bf16[2,64,1024]{2,1,0:T(8,128)(2,1)}, bf16[2,64,1024]{2,1,0:T(8,128)(2,1)S(1)}, u32[]{:S(2)}, u32[]{:S(2)}) collective-permute-start(bf16[2,64,1024]{2,1,0:T(8,128)(2,1)} %collective-permute-done.13), channel_id=1, source_target_pairs={{0,1},{1,0},{2,3},{3,2},{4,5},{5,4},{6,7},{7,6},{8,9},{9,8},{10,11... | collective-permute-start | bytes 786440 | tf_op jit(solution)/shard_map/ppermute | solution.py:260
  286.5 104.9 %collective-permute-start.51 = (bf16[4,128,1024]{2,1,0:T(8,128)(2,1)}, bf16[4,128,1024]{2,1,0:T(8,128)(2,1)}, u32[]{:S(2)}, u32[]{:S(2)}) collective-permute-start(bf16[4,128,1024]{2,1,0:T(8,128)(2,1)} %dynamic-slice_bitcast_fusion.1), channel_id=1, source_target_pairs={{0,4},{4,0},{8,12},{12,8},{16,20},{20,16},{24,28},{28,24},{1,5},{5... | collective-permute-start | bytes 3145736 | tf_op jit(solution)/shard_map/ppermute | solution.py:263
  292.4 103.5 %collective-permute-start.55 = (bf16[4,1024,128]{1,2,0:T(8,128)(2,1)}, bf16[4,1024,128]{1,2,0:T(8,128)(2,1)}, u32[]{:S(2)}, u32[]{:S(2)}) collective-permute-start(bf16[4,1024,128]{1,2,0:T(8,128)(2,1)} %dynamic-slice_bitcast_fusion), channel_id=1, source_target_pairs={{0,4},{4,0},{8,12},{12,8},{16,20},{20,16},{24,28},{28,24},{1,5},{5... | collective-permute-start | bytes 3145736 | tf_op jit(solution)/shard_map/ppermute | solution.py:263
  294.9 29.4 %collective-permute-start.16 = (bf16[2,64,1024]{2,1,0:T(8,128)(2,1)}, bf16[2,64,1024]{2,1,0:T(8,128)(2,1)}, u32[]{:S(2)}, u32[]{:S(2)}) collective-permute-start(bf16[2,64,1024]{2,1,0:T(8,128)(2,1)} %fusion.81), channel_id=1, source_target_pairs={{0,2},{1,3},{2,0},{3,1},{4,6},{5,7},{6,4},{7,5},{8,10},{9,11},{10,... | collective-permute-start | bytes 786440 | tf_op jit(solution)/shard_map/ppermute | solution.py:260
  312.9 24.3 %all-to-all-start.7 = ((bf16[4,2,16384]{2,1,0:T(2,128)(2,1)}), bf16[4,2,16384]{2,1,0:T(2,128)(2,1)}, u32[]{:S(2)}, u32[]{:S(2)}) async-start(bf16[4,2,16384]{2,1,0:T(2,128)(2,1)} %reshape.488), calls=%async_computation.7 | async-start | bytes 524288 | tf_op jit(solution)/shard_map/all_to_all | solution.py:536
  317.0 347.5 %all-gather.19.cloned.1.call-start = ((), (), s32[]{:S(2)}) async-start(), calls=%async_computation.13 | async-start | bytes 1310720 | tf_op jit(solution)/shard_map/all_gather | solution.py:525
  337.2 12.3 %all-to-all-start.6 = ((bf16[4,2,16384]{2,1,0:T(2,128)(2,1)}), bf16[4,2,16384]{2,1,0:T(2,128)(2,1)}, u32[]{:S(2)}, u32[]{:S(2)}) async-start(bf16[4,2,16384]{2,1,0:T(2,128)(2,1)} %reshape.490), calls=%async_computation.6 | async-start | bytes 524288 | tf_op jit(solution)/shard_map/all_to_all | solution.py:540
  349.5 14.0 %all-to-all-start.9 = ((f32[1,2,2,16,4,256]{5,3,2,1,0,4:T(8,128)}), f32[1,2,2,16,4,256]{5,3,2,1,0,4:T(8,128)}, u32[]{:S(2)}, u32[]{:S(2)}) async-start(f32[1,2,2,16,4,256]{5,3,2,1,0,4:T(8,128)} %copy.414), calls=%async_computation.9 | async-start | bytes 524288 | tf_op jit(solution)/shard_map/all_to_all | solution.py:518
  360.7 90.5 %collective-permute-start.22 = (bf16[2,2,256,256]{3,2,1,0:T(8,128)(2,1)}, bf16[2,2,256,256]{3,2,1,0:T(8,128)(2,1)}, u32[]{:S(2)}, u32[]{:S(2)}) collective-permute-start(bf16[2,2,256,256]{3,2,1,0:T(8,128)(2,1)} %pad_maximum_fusion.8), channel_id=1, source_target_pairs={{0,1},{1,0},{2,3},{3,2},{4,5},{5,4},{6,7},{7,6},{8,9},{9,8},{10,11... | collective-permute-start | bytes 1572872 | tf_op jit(solution)/shard_map/ppermute | solution.py:260
  363.5 47.6 %all-to-all-start.10 = ((bf16[4,2,32768]{2,1,0:T(2,128)(2,1)}), bf16[4,2,32768]{2,1,0:T(2,128)(2,1)}, u32[]{:S(2)}, u32[]{:S(2)}) async-start(bf16[4,2,32768]{2,1,0:T(2,128)(2,1)} %reshape.492), calls=%async_computation.10 | async-start | bytes 1048576 | tf_op jit(solution)/shard_map/all_to_all | solution.py:522
  395.9 42.0 %collective-permute-start.54 = (bf16[128,1024]{1,0:T(8,128)(2,1)}, bf16[128,1024]{1,0:T(8,128)(2,1)}, u32[]{:S(2)}, u32[]{:S(2)}) collective-permute-start(bf16[128,1024]{1,0:T(8,128)(2,1)} %get-tuple-element.153), channel_id=1, source_target_pairs={{0,24},{4,28},{8,16},{12,20},{16,8},{20,12},{24,0},{28,4},{1,25},{... | collective-permute-start | bytes 786440 | tf_op jit(solution)/shard_map/ppermute | solution.py:263
  403.1 15.9 %collective-permute-start.58 = (bf16[1024,128]{1,0:T(8,128)(2,1)}, bf16[1024,128]{1,0:T(8,128)(2,1)}, u32[]{:S(2)}, u32[]{:S(2)}) collective-permute-start(bf16[1024,128]{1,0:T(8,128)(2,1)} %bitcast.235), channel_id=1, source_target_pairs={{0,24},{4,28},{8,16},{12,20},{16,8},{20,12},{24,0},{28,4},{1,25},{... | collective-permute-start | bytes 786440 | tf_op jit(solution)/shard_map/ppermute | solution.py:263
  408.8 26.8 %collective-permute-start.57 = (bf16[1024,128]{1,0:T(8,128)(2,1)}, bf16[1024,128]{1,0:T(8,128)(2,1)}, u32[]{:S(2)}, u32[]{:S(2)}) collective-permute-start(bf16[1024,128]{1,0:T(8,128)(2,1)} %bitcast.234), channel_id=1, source_target_pairs={{0,16},{4,20},{8,24},{12,28},{16,0},{20,4},{24,8},{28,12},{1,17},{... | collective-permute-start | bytes 786440 | tf_op jit(solution)/shard_map/ppermute | solution.py:263
  410.5 25.0 %collective-permute-start.56 = (bf16[1024,128]{1,0:T(8,128)(2,1)}, bf16[1024,128]{1,0:T(8,128)(2,1)}, u32[]{:S(2)}, u32[]{:S(2)}) collective-permute-start(bf16[1024,128]{1,0:T(8,128)(2,1)} %bitcast.233), channel_id=1, source_target_pairs={{0,8},{4,12},{8,0},{12,4},{16,24},{20,28},{24,16},{28,20},{1,9},{5... | collective-permute-start | bytes 786440 | tf_op jit(solution)/shard_map/ppermute | solution.py:263
  419.1 21.8 %collective-permute-start.53 = (bf16[128,1024]{1,0:T(8,128)(2,1)S(1)}, bf16[128,1024]{1,0:T(8,128)(2,1)S(1)}, u32[]{:S(2)}, u32[]{:S(2)}) collective-permute-start(bf16[128,1024]{1,0:T(8,128)(2,1)S(1)} %copy-done.67), channel_id=1, source_target_pairs={{0,16},{4,20},{8,24},{12,28},{16,0},{20,4},{24,8},{28,12},{1,17},{... | collective-permute-start | bytes 786440 | tf_op jit(solution)/shard_map/ppermute | solution.py:263
  435.6 10.8 %collective-permute-start.52 = (bf16[128,1024]{1,0:T(8,128)(2,1)S(1)}, bf16[128,1024]{1,0:T(8,128)(2,1)S(1)}, u32[]{:S(2)}, u32[]{:S(2)}) collective-permute-start(bf16[128,1024]{1,0:T(8,128)(2,1)S(1)} %copy-done.66), channel_id=1, source_target_pairs={{0,8},{4,12},{8,0},{12,4},{16,24},{20,28},{24,16},{28,20},{1,9},{5... | collective-permute-start | bytes 786440 | tf_op jit(solution)/shard_map/ppermute | solution.py:263
  435.6 12.9 %collective-permute-start.39 = (bf16[4,128,256]{2,1,0:T(8,128)(2,1)S(1)}, bf16[4,128,256]{2,1,0:T(8,128)(2,1)S(1)}, u32[]{:S(2)}, u32[]{:S(2)}) collective-permute-start(bf16[4,128,256]{2,1,0:T(8,128)(2,1)S(1)} %dynamic-slice_bitcast_fusion.6), channel_id=1, source_target_pairs={{0,4},{4,0},{8,12},{12,8},{16,20},{20,16},{24,28},{28,24},{1,5},{5... | collective-permute-start | bytes 786440 | tf_op jit(solution)/shard_map/ppermute | solution.py:263
  437.9 18.2 %collective-permute-start.31 = (bf16[4,2,128,256]{3,2,1,0:T(8,128)(2,1)S(1)}, bf16[4,2,128,256]{3,2,1,0:T(8,128)(2,1)S(1)}, u32[]{:S(2)}, u32[]{:S(2)}) collective-permute-start(bf16[4,2,128,256]{3,2,1,0:T(8,128)(2,1)S(1)} %bitcast.727), channel_id=1, source_target_pairs={{0,4},{4,0},{8,12},{12,8},{16,20},{20,16},{24,28},{28,24},{1,5},{5... | collective-permute-start | bytes 1572872 | tf_op jit(solution)/shard_map/ppermute | solution.py:263
  440.9 24.9 %collective-permute-start.43 = (bf16[4,2,128,256]{3,2,1,0:T(8,128)(2,1)S(1)}, bf16[4,2,128,256]{3,2,1,0:T(8,128)(2,1)S(1)}, u32[]{:S(2)}, u32[]{:S(2)}) collective-permute-start(bf16[4,2,128,256]{3,2,1,0:T(8,128)(2,1)S(1)} %bitcast.726), channel_id=1, source_target_pairs={{0,4},{4,0},{8,12},{12,8},{16,20},{20,16},{24,28},{28,24},{1,5},{5... | collective-permute-start | bytes 1572872 | tf_op jit(solution)/shard_map/ppermute | solution.py:263
  448.6 19.9 %collective-permute-start.42 = (bf16[128,256]{1,0:T(8,128)(2,1)S(1)}, bf16[128,256]{1,0:T(8,128)(2,1)S(1)}, u32[]{:S(2)}, u32[]{:S(2)}) collective-permute-start(bf16[128,256]{1,0:T(8,128)(2,1)S(1)} %get-tuple-element.192), channel_id=1, source_target_pairs={{0,24},{4,28},{8,16},{12,20},{16,8},{20,12},{24,0},{28,4},{1,25},{... | collective-permute-start | bytes 196616 | tf_op jit(solution)/shard_map/ppermute | solution.py:263
  451.1 18.1 %collective-permute-start.41 = (bf16[128,256]{1,0:T(8,128)(2,1)S(1)}, bf16[128,256]{1,0:T(8,128)(2,1)S(1)}, u32[]{:S(2)}, u32[]{:S(2)}) collective-permute-start(bf16[128,256]{1,0:T(8,128)(2,1)S(1)} %get-tuple-element.193), channel_id=1, source_target_pairs={{0,16},{4,20},{8,24},{12,28},{16,0},{20,4},{24,8},{28,12},{1,17},{... | collective-permute-start | bytes 196616 | tf_op jit(solution)/shard_map/ppermute | solution.py:263
  451.2 19.4 %collective-permute-start.40 = (bf16[128,256]{1,0:T(8,128)(2,1)S(1)}, bf16[128,256]{1,0:T(8,128)(2,1)S(1)}, u32[]{:S(2)}, u32[]{:S(2)}) collective-permute-start(bf16[128,256]{1,0:T(8,128)(2,1)S(1)} %get-tuple-element.191), channel_id=1, source_target_pairs={{0,8},{4,12},{8,0},{12,4},{16,24},{20,28},{24,16},{28,20},{1,9},{5... | collective-permute-start | bytes 196616 | tf_op jit(solution)/shard_map/ppermute | solution.py:263
  456.1 35.9 %collective-permute-start.23 = (bf16[2,256,256]{2,1,0:T(8,128)(2,1)S(1)}, bf16[2,256,256]{2,1,0:T(8,128)(2,1)S(1)}, u32[]{:S(2)}, u32[]{:S(2)}) collective-permute-start(bf16[2,256,256]{2,1,0:T(8,128)(2,1)S(1)} %fusion.56), channel_id=1, source_target_pairs={{0,2},{1,3},{2,0},{3,1},{4,6},{5,7},{6,4},{7,5},{8,10},{9,11},{10,... | collective-permute-start | bytes 786440 | tf_op jit(solution)/shard_map/ppermute | solution.py:260
  468.5 15.9 %collective-permute-start.33 = (bf16[2,128,256]{2,1,0:T(8,128)(2,1)S(1)}, bf16[2,128,256]{2,1,0:T(8,128)(2,1)S(1)}, u32[]{:S(2)}, u32[]{:S(2)}) collective-permute-start(bf16[2,128,256]{2,1,0:T(8,128)(2,1)S(1)} %get-tuple-element.180), channel_id=1, source_target_pairs={{0,16},{4,20},{8,24},{12,28},{16,0},{20,4},{24,8},{28,12},{1,17},{... | collective-permute-start | bytes 393224 | tf_op jit(solution)/shard_map/ppermute | solution.py:263
  469.3 15.1 %collective-permute-start.32 = (bf16[2,128,256]{2,1,0:T(8,128)(2,1)S(1)}, bf16[2,128,256]{2,1,0:T(8,128)(2,1)S(1)}, u32[]{:S(2)}, u32[]{:S(2)}) collective-permute-start(bf16[2,128,256]{2,1,0:T(8,128)(2,1)S(1)} %get-tuple-element.178), channel_id=1, source_target_pairs={{0,8},{4,12},{8,0},{12,4},{16,24},{20,28},{24,16},{28,20},{1,9},{5... | collective-permute-start | bytes 393224 | tf_op jit(solution)/shard_map/ppermute | solution.py:263
  470.5 14.6 %collective-permute-start.46 = (bf16[2,128,256]{2,1,0:T(8,128)(2,1)S(1)}, bf16[2,128,256]{2,1,0:T(8,128)(2,1)S(1)}, u32[]{:S(2)}, u32[]{:S(2)}) collective-permute-start(bf16[2,128,256]{2,1,0:T(8,128)(2,1)S(1)} %get-tuple-element.176), channel_id=1, source_target_pairs={{0,24},{4,28},{8,16},{12,20},{16,8},{20,12},{24,0},{28,4},{1,25},{... | collective-permute-start | bytes 393224 | tf_op jit(solution)/shard_map/ppermute | solution.py:263
  474.1 16.3 %collective-permute-start.45 = (bf16[2,128,256]{2,1,0:T(8,128)(2,1)S(1)}, bf16[2,128,256]{2,1,0:T(8,128)(2,1)S(1)}, u32[]{:S(2)}, u32[]{:S(2)}) collective-permute-start(bf16[2,128,256]{2,1,0:T(8,128)(2,1)S(1)} %get-tuple-element.177), channel_id=1, source_target_pairs={{0,16},{4,20},{8,24},{12,28},{16,0},{20,4},{24,8},{28,12},{1,17},{... | collective-permute-start | bytes 393224 | tf_op jit(solution)/shard_map/ppermute | solution.py:263
  493.5 65.2 %collective-permute-start.24 = (bf16[2,272,256]{2,1,0:T(8,128)(2,1)}, bf16[2,272,256]{2,1,0:T(8,128)(2,1)}, u32[]{:S(2)}, u32[]{:S(2)}) collective-permute-start(bf16[2,272,256]{2,1,0:T(8,128)(2,1)} %pad_maximum_fusion.11), channel_id=1, source_target_pairs={{0,4},{4,0},{8,12},{12,8},{16,20},{20,16},{24,28},{28,24},{1,5},{5... | collective-permute-start | bytes 835592 | tf_op jit(solution)/shard_map/ppermute | solution.py:263
  493.7 65.9 %collective-permute-start.25 = (bf16[2,272,256]{2,1,0:T(8,128)(2,1)}, bf16[2,272,256]{2,1,0:T(8,128)(2,1)}, u32[]{:S(2)}, u32[]{:S(2)}) collective-permute-start(bf16[2,272,256]{2,1,0:T(8,128)(2,1)} %pad_maximum_fusion.11), channel_id=1, source_target_pairs={{0,8},{4,12},{8,0},{12,4},{16,24},{20,28},{24,16},{28,20},{1,9},{5... | collective-permute-start | bytes 835592 | tf_op jit(solution)/shard_map/ppermute | solution.py:263
  493.7 68.1 %collective-permute-start.26 = (bf16[2,272,256]{2,1,0:T(8,128)(2,1)}, bf16[2,272,256]{2,1,0:T(8,128)(2,1)}, u32[]{:S(2)}, u32[]{:S(2)}) collective-permute-start(bf16[2,272,256]{2,1,0:T(8,128)(2,1)} %pad_maximum_fusion.11), channel_id=1, source_target_pairs={{0,12},{4,8},{8,4},{12,0},{16,28},{20,24},{24,20},{28,16},{1,13},{... | collective-permute-start | bytes 835592 | tf_op jit(solution)/shard_map/ppermute | solution.py:263
  497.0 65.9 %collective-permute-start.27 = (bf16[2,272,256]{2,1,0:T(8,128)(2,1)}, bf16[2,272,256]{2,1,0:T(8,128)(2,1)}, u32[]{:S(2)}, u32[]{:S(2)}) collective-permute-start(bf16[2,272,256]{2,1,0:T(8,128)(2,1)} %pad_maximum_fusion.11), channel_id=1, source_target_pairs={{0,16},{4,20},{8,24},{12,28},{16,0},{20,4},{24,8},{28,12},{1,17},{... | collective-permute-start | bytes 835592 | tf_op jit(solution)/shard_map/ppermute | solution.py:263
  497.8 66.0 %collective-permute-start.28 = (bf16[2,272,256]{2,1,0:T(8,128)(2,1)}, bf16[2,272,256]{2,1,0:T(8,128)(2,1)}, u32[]{:S(2)}, u32[]{:S(2)}) collective-permute-start(bf16[2,272,256]{2,1,0:T(8,128)(2,1)} %pad_maximum_fusion.11), channel_id=1, source_target_pairs={{0,20},{4,16},{8,28},{12,24},{16,4},{20,0},{24,12},{28,8},{1,21},{... | collective-permute-start | bytes 835592 | tf_op jit(solution)/shard_map/ppermute | solution.py:263
  558.7 11.6 %collective-permute-start.29 = (bf16[2,272,256]{2,1,0:T(8,128)(2,1)}, bf16[2,272,256]{2,1,0:T(8,128)(2,1)S(1)}, u32[]{:S(2)}, u32[]{:S(2)}) collective-permute-start(bf16[2,272,256]{2,1,0:T(8,128)(2,1)} %pad_maximum_fusion.11), channel_id=1, source_target_pairs={{0,24},{4,28},{8,16},{12,20},{16,8},{20,12},{24,0},{28,4},{1,25},{... | collective-permute-start | bytes 835592 | tf_op jit(solution)/shard_map/ppermute | solution.py:263
  559.7 13.3 %collective-permute-start.30 = (bf16[2,272,256]{2,1,0:T(8,128)(2,1)}, bf16[2,272,256]{2,1,0:T(8,128)(2,1)S(1)}, u32[]{:S(2)}, u32[]{:S(2)}) collective-permute-start(bf16[2,272,256]{2,1,0:T(8,128)(2,1)} %pad_maximum_fusion.11), channel_id=1, source_target_pairs={{0,28},{4,24},{8,20},{12,16},{16,12},{20,8},{24,4},{28,0},{1,29},{... | collective-permute-start | bytes 835592 | tf_op jit(solution)/shard_map/ppermute | solution.py:263
  590.0 102.7 %all-to-all-start.8 = ((f32[32,1,4096]{2,1,0:T(1,128)}), f32[32,1,4096]{2,1,0:T(1,128)S(1)}, u32[]{:S(2)}, u32[]{:S(2)}) async-start(f32[32,1,4096]{2,1,0:T(1,128)} %bitcast.134), calls=%async_computation.8 | async-start | bytes 1048576 | tf_op jit(solution)/shard_map/all_to_all | solution.py:586
  666.3 12.4 %collective-permute-start.47 = (bf16[4,256,128]{1,2,0:T(8,128)(2,1)S(1)}, bf16[4,256,128]{1,2,0:T(8,128)(2,1)S(1)}, u32[]{:S(2)}, u32[]{:S(2)}) collective-permute-start(bf16[4,256,128]{1,2,0:T(8,128)(2,1)S(1)} %dynamic-slice_bitcast_fusion.5), channel_id=1, source_target_pairs={{0,4},{4,0},{8,12},{12,8},{16,20},{20,16},{24,28},{28,24},{1,5},{5... | collective-permute-start | bytes 786440 | tf_op jit(solution)/shard_map/ppermute | solution.py:263
  679.1 9.7 %collective-permute-start.37 = (bf16[256,128]{1,0:T(8,128)(2,1)S(1)}, bf16[256,128]{1,0:T(8,128)(2,1)S(1)}, u32[]{:S(2)}, u32[]{:S(2)}) collective-permute-start(bf16[256,128]{1,0:T(8,128)(2,1)S(1)} %bitcast.746), channel_id=1, source_target_pairs={{0,16},{4,20},{8,24},{12,28},{16,0},{20,4},{24,8},{28,12},{1,17},{... | collective-permute-start | bytes 196616 | tf_op jit(solution)/shard_map/ppermute | solution.py:263
  679.3 9.5 %collective-permute-start.36 = (bf16[256,128]{1,0:T(8,128)(2,1)S(1)}, bf16[256,128]{1,0:T(8,128)(2,1)S(1)}, u32[]{:S(2)}, u32[]{:S(2)}) collective-permute-start(bf16[256,128]{1,0:T(8,128)(2,1)S(1)} %bitcast.748), channel_id=1, source_target_pairs={{0,8},{4,12},{8,0},{12,4},{16,24},{20,28},{24,16},{28,20},{1,9},{5... | collective-permute-start | bytes 196616 | tf_op jit(solution)/shard_map/ppermute | solution.py:263
  (133 other events, 1474.2 us)
Sparse Core Ops, SparseCore 0:
  10.8 43.3 all-gather.22
  56.3 54.7 all-gather.20
  125.7 101.1 all-gather.24
  259.7 15.9 all-gather.16
  306.3 15.8 all-gather.14
  337.4 16.9 all-gather.18
